TPU v7x, 256 devices: a whole 4x4x8 slice. The times are simulated.
256 devices in a mesh: ph: 4 (over x_lo, core), ka: 64 (over x_hi, z, y).
Axes of the slice: x: 4 (x_hi: 2, x_lo: 2; x = x_hi * 2 + x_lo), y: 4, z: 8, core: 2. Of those that a mesh axis runs over, the one named last changes fastest.
Arguments:
- g_wan: bfloat16 [256, 48, 48, 2, 1024], P('ka', 'ph'), may hold values from -6 to 6
- el_cells: int32 [3, 256], replicated, may hold values from -6 to 6
- ph_cells: int32 [3, 48], P(None, 'ph'), may hold values from -4 to 4
- q_point: int32 [3], replicated, may hold values from 0 to 63
- kpoints: int32 [3, 16384], P(None, 'ka'), may hold values from 0 to 63
- eigvec: float32 [2, 48, 48], replicated, may hold values from -0.875 to 0.875
- omega: float32 [48], replicated, may hold values from 0.25 to 4
Outputs:
- strength: float32 [48, 32, 16384], P('ph', None, 'ka')
All inputs are finite; a program needn't handle non-finite values.
Results may differ from a plain program's by a relative error of at most 0.0018.
Values may be sent and summed in bfloat16 or wider, within the bound.
No kernel may reach another device: no remote copies, remote signals or barrier semaphores. Data moves between devices by JAX's collectives and lax.ppermute only.
A program may use at most 128 MiB of HBM per device.

v0:
```python
import math

import jax
import jax.numpy as jnp
from jax import lax
from jax.sharding import PartitionSpec as P

W = 32
KGRID = 64


def angles(numerators, vectors):
    summed = jnp.sum(numerators[:, :, None] * vectors[:, None, :], axis=0)
    return jnp.mod(summed, KGRID).astype(jnp.float32) * (2.0 * math.pi / KGRID)


def coupling(q_angle, eigvec, omega):
    mode_scale = 1.0 / jnp.sqrt(2.0 * omega)
    cos_phase = jnp.cos(q_angle)[:, None, None]
    sin_phase = jnp.sin(q_angle)[:, None, None]
    real_part = eigvec[0][None]
    imag_part = eigvec[1][None]
    coef_re = ((cos_phase * real_part - sin_phase * imag_part) * mode_scale).astype(jnp.bfloat16)
    coef_im = ((sin_phase * real_part + cos_phase * imag_part) * mode_scale).astype(jnp.bfloat16)
    return jnp.stack([jnp.stack([coef_re, coef_im], 2), jnp.stack([-coef_im, coef_re], 2)], 2)


def stacked(mode_block):
    row_count = mode_block.shape[0]
    vert_re = mode_block[:, :, 0, :].reshape(row_count, -1)
    vert_im = mode_block[:, :, 1, :].reshape(row_count, -1)
    upper = jnp.concatenate([vert_re, vert_im], 1)
    lower = jnp.concatenate([-vert_im, vert_re], 1)
    return jnp.concatenate([upper, lower], 0)


def pair_strength(bloch_sum, mode_count, normalizer):
    k_count = bloch_sum.shape[0]
    half_width = bloch_sum.shape[1] // 2
    bloch_re = bloch_sum[:, :half_width].reshape(k_count, mode_count, W, W)
    bloch_im = bloch_sum[:, half_width:].reshape(k_count, mode_count, W, W)
    summed = jnp.sum(bloch_re * bloch_re + bloch_im * bloch_im, axis=3) / normalizer
    return summed.transpose(1, 2, 0)


def shards(g_wan, el_cells, ph_cells, q_point, kpoints, eigvec, omega):
    q_angle = angles(q_point[:, None], ph_cells)[0]
    coupling_table = coupling(q_angle, eigvec, omega)
    partial_terms = jnp.einsum(
        "pncom,epncw->emow", coupling_table, g_wan, preferred_element_type=jnp.float32
    )
    mode_vertex = lax.psum_scatter(partial_terms, "ph", scatter_dimension=1, tiled=True).astype(
        jnp.bfloat16
    )
    k_angle = angles(kpoints, el_cells)
    phase_cos = jnp.cos(k_angle).astype(jnp.bfloat16)
    phase_sin = jnp.sin(k_angle).astype(jnp.bfloat16)
    phase_left = jnp.concatenate([phase_cos, phase_sin], 1)
    cell_total = el_cells.shape[1]
    normalizer = float(cell_total * g_wan.shape[1] * lax.axis_size("ph") * W)
    results = []
    for offset in range(0, mode_vertex.shape[1], 4):
        mode_block = mode_vertex[:, offset : offset + 4]
        gathered = lax.all_gather(mode_block, "ka", axis=0, tiled=True)
        bloch_sum = jnp.dot(phase_left, stacked(gathered), preferred_element_type=jnp.float32)
        results.append(pair_strength(bloch_sum, 4, normalizer))
    return jnp.concatenate(results, 0)


def solution(mesh):
    return jax.shard_map(
        shards,
        mesh=mesh,
        in_specs=(
            P("ka", "ph", None, None, None),
            P(),
            P(None, "ph"),
            P(),
            P(None, "ka"),
            P(),
            P(),
        ),
        out_specs=P("ph", None, "ka"),
        check_vma=False,
    )
```

profile of v0, /device:TPU:6, one launch (start us, length us, event | category | flops | bytes accessed | tf_op | source)
XLA Modules:
  0.0 480.9 jit_solution(12905698075399148672)
XLA Ops:
  6.5 0.0 all-gather.6.cloned.1.call-start
  6.5 0.8 slice_bitcast_fusion.1
  7.3 0.1 copy.53
  7.4 0.1 copy.54
  7.4 0.8 multiply_reduce_fusion.1
  8.2 0.1 fusion.46
  8.3 0.7 multiply_rsqrt_fusion
  9.0 0.2 multiply_convert_fusion
  9.2 0.1 fusion.45
  9.4 0.1 maximum_bitcast_fusion.2
  9.5 7.1 %fusion.30 = f32[4,48,2,1024]{3,1,0,2:T(8,128)S(1)} fusion(bf16[4,12,48,2,1024]{4,3,2,1,0:T(2,128)(2,1)} %param.7, bf16[12,48,1,2,48]{1,4,0,2,3:T(8,128)(2,1)S(1)} %get-tuple-element.19, bf16[12,48,1,2,48]{1,4,0,2,3:T(8,128)(2,1)S(1)} %get-tuple-element.18), kind=kOutput, calls=%fused_computation.39 | convolution fusion | flops 906412032 | bytes 11231232 | tf_op jit(solution)/shard_map/pncom,epncw->emow/dot_general | solution.py:49
  16.7 0.0 copy-start.3
  16.7 0.0 copy-start.1
  16.7 0.0 copy-start.2
  16.7 1.0 copy.57
  17.7 32.7 %all-reduce.2 = bf16[4,48,2,1024]{3,0,2,1:T(4,128)(2,1)S(1)} all-reduce(f32[4,48,2,1024]{3,0,2,1:T(4,128)S(1)} %copy.57), channel_id=2, replica_groups=mesh['ph'=4,'ka'=64] {'ph'}, use_global_device_ids=true, to_apply=%region_2.3.clone | all-reduce | flops 393216 | bytes 2359296
  50.4 0.0 copy-done.3
  50.4 0.6 dynamic-slice
  51.7 0.1 dynamic-slice_convert_fusion
  51.7 0.1 fusion.51
  51.8 0.7 copy.62
  52.5 0.0 all-gather.6.cloned.1.call-update
  52.5 0.0 all-gather.8.cloned.1.call-start
  52.6 0.7 copy.66
  53.3 0.0 all-gather.8.cloned.1.call-update
  53.3 0.2 all-gather.4.cloned.1.call-start
  53.5 0.7 copy.58
  54.2 0.0 all-gather.4.cloned.1.call-update
  54.2 0.0 copy-done.1
  54.2 0.0 copy-done.2
  54.2 0.2 multiply_reduce_fusion
  54.4 1.1 cosine_convert_fusion
  55.5 126.0 %all-gather.6.cloned.1.call-done = bf16[256,4,2,1024]{3,1,2,0:T(4,128)(2,1)} async-done(((bf16[4,4,2,1024]{3,1,2,0:T(4,128)(2,1)}), bf16[256,4,2,1024]{3,1,2,0:T(4,128)(2,1)}) %all-gather.6.cloned.1.call-update) | async-done | bytes 4194320 | tf_op jit(solution)/shard_map/all_gather | solution.py:64
  181.5 4.3 fusion.49
  185.8 3.0 copy.75
  188.8 4.3 copy.74
  193.1 1.6 bitcast_negate_fusion.1
  194.7 12.1 %fusion.11 = f32[256,8192]{1,0:T(8,128)S(1)} fusion(bf16[256,4096]{0,1:T(8,128)(2,1)} %bitcast.52, bf16[256,4096]{0,1:T(8,128)(2,1)} %bitcast_negate_fusion.1, bf16[256,4096]{0,1:T(8,128)(2,1)S(1)} %bitcast.49, bf16[256,256]{1,0:T(8,128)(2,1)S(1)} %get-tuple-element.14, bf16[256,256]{1,0:T(8,128)(2,1)S(1)} %get-tuple-element.13), kind=kOutput, calls=%fused_computation.11 | convolution fusion | flops 2181562368 | bytes 14942208 | tf_op jit(solution)/shard_map/dot_general | solution.py:65
  206.8 2.6 fusion.28
  209.4 5.6 %copy.65 = f32[256,4096]{0,1:T(8,128)} copy(f32[256,4096]{1,0:T(8,128)} %fusion.28) | data formatting | bytes 8388608 | tf_op jit(solution)/shard_map/add | solution.py:42
  215.0 94.3 %all-gather.8.cloned.1.call-done = bf16[256,4,2,1024]{3,1,2,0:T(4,128)(2,1)} async-done(((bf16[4,4,2,1024]{3,1,2,0:T(4,128)(2,1)}), bf16[256,4,2,1024]{3,1,2,0:T(4,128)(2,1)}) %all-gather.8.cloned.1.call-update) | async-done | bytes 4194320 | tf_op jit(solution)/shard_map/all_gather | solution.py:64
  309.3 4.3 fusion.50
  313.6 3.0 copy.77
  316.6 4.2 copy.76
  320.9 1.6 bitcast_negate_fusion
  322.5 12.1 %fusion.19 = f32[256,8192]{1,0:T(8,128)S(1)} fusion(bf16[256,4096]{0,1:T(8,128)(2,1)} %bitcast.53, bf16[256,4096]{0,1:T(8,128)(2,1)} %bitcast_negate_fusion, bf16[256,4096]{0,1:T(8,128)(2,1)S(1)} %bitcast.50, bf16[256,256]{1,0:T(8,128)(2,1)S(1)} %get-tuple-element.14, bf16[256,256]{1,0:T(8,128)(2,1)S(1)} %get-tuple-element.13), kind=kOutput, calls=%fused_computation.19 | convolution fusion | flops 2181562368 | bytes 14942208 | tf_op jit(solution)/shard_map/dot_general | solution.py:65
  334.6 2.6 fusion.27
  337.2 5.6 %copy.69 = f32[256,4096]{0,1:T(8,128)} copy(f32[256,4096]{1,0:T(8,128)} %fusion.27) | data formatting | bytes 8388608 | tf_op jit(solution)/shard_map/add | solution.py:42
  342.8 0.0 copy-start
  342.8 3.0 bitcast_reduce_fusion.1
  345.9 0.4 copy-done
  346.3 0.7 bitcast_reduce_fusion
  347.0 90.1 %all-gather.4.cloned.1.call-done = bf16[256,4,2,1024]{3,1,2,0:T(4,128)(2,1)} async-done(((bf16[4,4,2,1024]{3,1,2,0:T(4,128)(2,1)}), bf16[256,4,2,1024]{3,1,2,0:T(4,128)(2,1)}) %all-gather.4.cloned.1.call-update) | async-done | bytes 4194320 | tf_op jit(solution)/shard_map/all_gather | solution.py:64
  437.1 4.4 fusion.48
  441.5 3.0 copy.73
  444.5 1.6 bitcast_negate_fusion.2
  446.1 4.3 copy.72
  450.4 12.1 %fusion.3 = f32[256,8192]{1,0:T(8,128)S(1)} fusion(bf16[256,4096]{0,1:T(8,128)(2,1)} %bitcast.51, bf16[256,4096]{0,1:T(8,128)(2,1)} %bitcast_negate_fusion.2, bf16[256,4096]{0,1:T(8,128)(2,1)S(1)} %bitcast.48, bf16[256,256]{1,0:T(8,128)(2,1)S(1)} %get-tuple-element.14, bf16[256,256]{1,0:T(8,128)(2,1)S(1)} %get-tuple-element.13), kind=kOutput, calls=%fused_computation.3 | convolution fusion | flops 2181562368 | bytes 14942208 | tf_op jit(solution)/shard_map/dot_general | solution.py:65
  462.5 2.6 fusion.29
  465.1 5.6 %copy.61 = f32[256,4096]{0,1:T(8,128)} copy(f32[256,4096]{1,0:T(8,128)} %fusion.29) | data formatting | bytes 8388608 | tf_op jit(solution)/shard_map/add | solution.py:42
  470.7 2.9 bitcast_reduce_fusion.2
  473.6 0.8 pad_maximum_fusion
  (3 shorter events, 0.1 us)
Async XLA Ops:
  6.5 175.0 %all-gather.6.cloned.1.call-start = ((), (), s32[]{:S(2)}) async-start(), calls=%async_computation.1 | async-start | bytes 4259840 | tf_op jit(solution)/shard_map/all_gather | solution.py:64
  16.7 33.7 %copy-start.3 = (u32[256]{0:T(256)S(1)}, u32[256]{0:T(256)}, u32[]{:S(2)}) copy-start(u32[256]{0:T(256)} %constant.40) | copy-start | bytes 3076
  16.7 37.5 %copy-start.1 = (s32[3,256]{1,0:T(4,128)S(1)}, s32[3,256]{1,0:T(4,128)}, u32[]{:S(2)}) copy-start(s32[3,256]{1,0:T(4,128)} %param.8) | copy-start | bytes 9220
  16.7 37.5 %copy-start.2 = (s32[3,256]{1,0:T(4,128)S(1)}, s32[3,256]{1,0:T(4,128)}, u32[]{:S(2)}) copy-start(s32[3,256]{1,0:T(4,128)} %param.11) | copy-start | bytes 9220
  52.5 256.8 %all-gather.8.cloned.1.call-start = ((), (), s32[]{:S(2)}) async-start(), calls=%async_computation.2 | async-start | bytes 4259840 | tf_op jit(solution)/shard_map/all_gather | solution.py:64
  53.3 383.9 %all-gather.4.cloned.1.call-start = ((), (), s32[]{:S(2)}) async-start(), calls=%async_computation | async-start | bytes 4259840 | tf_op jit(solution)/shard_map/all_gather | solution.py:64
  342.8 3.5 copy-start
Sparse Core Ops, SparseCore 0:
  52.6 128.8 all-gather.5
  185.0 124.2 all-gather.7
  312.8 124.2 all-gather.3
where the time goes:
time: 483 us; the launch traced here: 481 us
  waiting for transfers between devices  310 us (64%)
  local copies, waits for them, and re-layouts  56.8 us (12%)
  matrix products  43.5 us (9%)
  blocking collectives  32.7 us (7%)
  other arithmetic  23.3 us (5%)
  between operations  14 us (3%)
    all_gather x3, waiting for transfers between devices, shards(): gathered = lax.all_gather(mode_block, 'ka', axis=0, tiled=True)  310 us
    dot_general x3, matrix products, shards(): jnp.dot(phase_left, stacked(gathered), preferred_element_type=jnp.float32)  36.3 us
    unnamed x1, blocking collectives  32.7 us
    unnamed x15, local copies, waits for them, and re-layouts  22.7 us
    add x3, local copies, waits for them, and re-layouts, pair_strength(): bloch_re * bloch_re + bloch_im * bloch_im  16.9 us
    slice x3, local copies, waits for them, and re-layouts, stacked(): vert_im = mode_block[:, :, 1, :].reshape(row_count, -1)  13 us
  transfers between devices with their start and end apart: 3, of which 3 were waited for; matrix products, arithmetic and copies ran while one was open for 15% of the time, Pallas kernels for 0%

commit v1 on v0

v1 whole, which is shorter than its diff:
```python
import math

import jax
import jax.numpy as jnp
from jax import lax
from jax.experimental import pallas as pl
from jax.experimental.pallas import tpu as pltpu
from jax.sharding import Mesh, PartitionSpec as P

W = 32
KGRID = 64
PH = ("xl", "core")
KA = ("xh", "z", "y")
SWAP = [(0, 1), (1, 0)]


def coupling(q_angle, eigvec, omega):
    mode_scale = 1.0 / jnp.sqrt(2.0 * omega)
    cos_phase = jnp.cos(q_angle)[:, None, None]
    sin_phase = jnp.sin(q_angle)[:, None, None]
    real_part = eigvec[0][None]
    imag_part = eigvec[1][None]
    coef_re = ((cos_phase * real_part - sin_phase * imag_part) * mode_scale).astype(jnp.bfloat16)
    coef_im = ((sin_phase * real_part + cos_phase * imag_part) * mode_scale).astype(jnp.bfloat16)
    return jnp.stack([jnp.stack([coef_re, coef_im], 2), jnp.stack([-coef_im, coef_re], 2)], 2)


def strength_kernel(modes, scale, kp_ref, el_ref, table_ref, vert_ref, out_ref, left, phase):
    cells = vert_ref.shape[0]
    width = kp_ref.shape[1]

    @pl.when(pl.program_id(0) == 0)
    def _():
        turned = vert_ref[...].astype(jnp.float32).T
        for m in range(modes):
            re = turned[m * 2 * W : m * 2 * W + W]
            im = turned[m * 2 * W + W : (m + 1) * 2 * W]
            rows = pl.ds(m * 2 * W, 2 * W)
            left[rows, :cells] = jnp.concatenate([re, im], 0).astype(jnp.bfloat16)
            left[rows, cells:] = jnp.concatenate([-im, re], 0).astype(jnp.bfloat16)

    numer = jnp.dot(el_ref[...], kp_ref[...], preferred_element_type=jnp.float32)
    index = numer.astype(jnp.int32) & 127
    for lane in range(0, width, 128):
        part = index[:, lane : lane + 128]
        cos_table = jnp.broadcast_to(table_ref[0:1, :], (cells, 128))
        sin_table = jnp.broadcast_to(table_ref[1:2, :], (cells, 128))
        cos = jnp.take_along_axis(cos_table, part, axis=1)
        sin = jnp.take_along_axis(sin_table, part, axis=1)
        phase[:cells, lane : lane + 128] = cos.astype(jnp.bfloat16)
        phase[cells:, lane : lane + 128] = sin.astype(jnp.bfloat16)
    bloch = jnp.dot(left[...], phase[...], preferred_element_type=jnp.float32)
    square = bloch * bloch
    total = jnp.sum(square.reshape(modes, 2 * W, width), axis=1) * scale
    for lane in range(0, width, 128):
        row = lane // 128 * modes
        out_ref[0, row : row + modes, :] = total[:, lane : lane + 128]


def strengths(kp, el, table, vert, modes, scale, dests):
    cells, cols = vert.shape
    width = kp.shape[1] // dests
    return pl.pallas_call(
        lambda *refs: strength_kernel(modes, scale, *refs),
        grid=(dests,),
        in_specs=[
            pl.BlockSpec((kp.shape[0], width), lambda i: (0, i)),
            pl.BlockSpec(el.shape, lambda i: (0, 0)),
            pl.BlockSpec(table.shape, lambda i: (0, 0)),
            pl.BlockSpec(vert.shape, lambda i: (0, 0)),
        ],
        out_specs=pl.BlockSpec((1, modes * width // 128, 128), lambda i: (i, 0, 0)),
        out_shape=jax.ShapeDtypeStruct((dests, modes * width // 128, 128), jnp.float32),
        scratch_shapes=[
            pltpu.VMEM((cols, 2 * cells), jnp.bfloat16),
            pltpu.VMEM((2 * cells, width), jnp.bfloat16),
        ],
        cost_estimate=pl.CostEstimate(
            flops=4 * cols * cells * kp.shape[1], bytes_accessed=2 * vert.size, transcendentals=0
        ),
        name="strengths",
    )(kp, el, table, vert)


def shards(g_wan, el_cells, ph_cells, q_point, kpoints, eigvec, omega):
    bf16, f32 = jnp.bfloat16, jnp.float32
    xl, core, xh = (lax.axis_index(a) for a in ("xl", "core", "xh"))
    e = g_wan.shape[0]
    k_dev = kpoints.shape[1]
    nu = eigvec.shape[1]
    modes = nu // 4
    unit = 2.0 * math.pi / KGRID
    q_sum = jnp.sum(q_point[:, None] * ph_cells, axis=0)
    q_angle = jnp.mod(q_sum, KGRID).astype(f32) * unit
    table = coupling(q_angle, eigvec, omega)
    partial = jnp.einsum("pncom,epncw->emow", table, g_wan, preferred_element_type=f32)
    partial = partial.reshape(e, 2, 2, modes, 2, W * W)
    mine = lax.dynamic_index_in_dim(partial, core, 2, keepdims=False)
    theirs = lax.dynamic_index_in_dim(partial, 1 - core, 2, keepdims=False)
    both = mine + lax.ppermute(theirs, "core", SWAP)
    mine = lax.dynamic_index_in_dim(both, xl, 1, keepdims=False)
    theirs = lax.dynamic_index_in_dim(both, 1 - xl, 1, keepdims=False).astype(bf16)
    vert = (mine + lax.ppermute(theirs, "xl", SWAP).astype(f32)).astype(bf16)
    vert = vert.reshape(e, 2 * modes, W, W).transpose(2, 0, 1, 3).reshape(W, -1, 128)
    kp = jnp.broadcast_to(kpoints.astype(bf16).reshape(1, -1, 128), (W, 3 * k_dev // 128, 128))
    rows = vert.shape[1]
    moved = lax.all_to_all(jnp.concatenate([vert, kp], 1), ("z", "y"), 0, 0, tiled=True)
    own = moved[:, :rows].reshape(W * e, 2 * modes * W)
    kp = moved[:, rows:].reshape(W, 3, k_dev).transpose(1, 0, 2).reshape(3, W * k_dev)
    other = lax.ppermute(own, "xh", SWAP)
    half = W * e
    el = el_cells.astype(bf16).T
    el = jnp.concatenate(
        [
            lax.dynamic_slice_in_dim(el, xh * half, half, 0),
            lax.dynamic_slice_in_dim(el, (1 - xh) * half, half, 0),
        ]
    )
    el = jnp.pad(el, ((0, 0), (0, 5)))
    kp = jnp.pad(kp, ((0, 5), (0, 0)))
    angle = (jnp.arange(128) % KGRID).astype(f32) * unit
    trig = jnp.stack([jnp.cos(angle), jnp.sin(angle)]).astype(bf16).astype(f32)
    trig = jnp.pad(trig, ((0, 6), (0, 0)))
    scale = 1.0 / float(el_cells.shape[1] * nu * W)
    found = strengths(kp, el, trig, jnp.concatenate([own, other]), modes, scale, W)
    found = lax.all_to_all(found, ("z", "y"), 0, 0, tiled=True)
    found = found.reshape(W, k_dev // 128, modes, 128).transpose(2, 0, 1, 3)
    return found.reshape(modes, W, k_dev)


def solution(mesh):
    split = Mesh(mesh.devices.reshape(2, 2, 2, 8, 4), PH + KA)
    return jax.shard_map(
        shards,
        mesh=split,
        in_specs=(
            P(KA, PH, None, None, None),
            P(),
            P(None, PH),
            P(),
            P(None, KA),
            P(),
            P(),
        ),
        out_specs=P(PH, None, KA),
        check_vma=False,
    )
```

time: 483 us -> 104 us (0.22)
  waiting for transfers between devices: 310 us -> 24.2 us
  local copies, waits for them, and re-layouts: 56.8 us -> 6.06 us
  matrix products: 43.5 us -> 7.14 us
  Pallas kernels: 0 us -> 28.9 us
  other arithmetic: 23.3 us -> 4.79 us
  blocking collectives: 32.7 us -> 17.9 us
  between operations: 14 us -> 0.21 us
  starting transfers between devices: 0.27 us -> 14 us
    all_gather x3 -> x0, waiting for transfers between devices: 310 us -> none  [shards(): gathered = lax.all_gather(mode_block, 'ka', axis=0, tiled=True)]
    dot_general x4 -> x1, matrix products: 43.5 us -> 7.14 us  [shards(): jnp.einsum('pncom,epncw->emow', table, g_wan, preferred_element_type=f32)]
    unnamed x1 -> x0, blocking collectives: 32.7 us -> none
    pallas_call x0 -> x1, Pallas kernels: none -> 28.9 us  [strengths(): pl.pallas_call(lambda *refs: strength_kernel(modes, scale, *refs), grid=(...]
    unnamed x15 -> x4, local copies, waits for them, and re-layouts: 22.7 us -> 0.01 us
    all_to_all x0 -> x1, blocking collectives: none -> 17.9 us  [shards(): found = lax.all_to_all(found, ('z', 'y'), 0, 0, tiled=True)]
    add x3 -> x0, local copies, waits for them, and re-layouts: 16.9 us -> none  [pair_strength(): bloch_re * bloch_re + bloch_im * bloch_im]
    slice x7 -> x2, local copies, waits for them, and re-layouts: 15.1 us -> 0.03 us  [the longest x1 0.02 us: shards(): own = moved[:, :rows].reshape(W * e, 2 * modes * W)]
  transfers between devices with their start and end apart: 3 -> 4, of which waited for: 3 -> 4; matrix products, arithmetic and copies ran while one was open for 15% -> 2% of each run, Pallas kernels for 0% -> 0%
where the time goes in v1:
time: 104 us; the launch traced here: 103 us
  Pallas kernels  28.9 us (28%)
  waiting for transfers between devices  24.2 us (23%)
  blocking collectives  17.9 us (17%)
  starting transfers between devices  14 us (13%)
  matrix products  7.14 us (7%)
  local copies, waits for them, and re-layouts  6.06 us (6%)
  other arithmetic  4.79 us (5%)
    pallas_call x1, Pallas kernels, strengths(): pl.pallas_call(lambda *refs: strength_kernel(modes, scale, *refs), grid=(...  28.9 us
    all_to_all x1, blocking collectives, shards(): found = lax.all_to_all(found, ('z', 'y'), 0, 0, tiled=True)  17.9 us
    all_to_all x1, starting transfers between devices, shards(): lax.all_to_all(jnp.concatenate([vert, kp], 1), ('z', 'y'), 0, 0, tiled=True)  11.5 us
    all_to_all x1, waiting for transfers between devices, shards(): lax.all_to_all(jnp.concatenate([vert, kp], 1), ('z', 'y'), 0, 0, tiled=True)  11.5 us
    dot_general x1, matrix products, shards(): jnp.einsum('pncom,epncw->emow', table, g_wan, preferred_element_type=f32)  7.14 us
    ppermute x1, waiting for transfers between devices, shards(): vert = (mine + lax.ppermute(theirs, 'xl', SWAP).astype(f32)).astype(bf16)  6.08 us
    ppermute x1, waiting for transfers between devices, shards(): other = lax.ppermute(own, 'xh', SWAP)  4.38 us
    ppermute x1, waiting for transfers between devices, shards(): both = mine + lax.ppermute(theirs, 'core', SWAP)  2.27 us
  transfers between devices with their start and end apart: 4, of which 4 were waited for; matrix products, arithmetic and copies ran while one was open for 2% of the time, Pallas kernels for 0%

profile of v1, /device:TPU:6, one launch (start us, length us, event | category | flops | bytes accessed | tf_op | source)
XLA Modules:
  0.0 103.2 jit_solution(18144962564684086716)
XLA Ops:
  0.0 0.8 slice_bitcast_fusion.1
  0.8 0.1 copy.31
  0.8 0.1 copy.32
  0.9 0.8 multiply_reduce_fusion
  1.7 0.1 fusion.23
  1.8 0.7 multiply_rsqrt_fusion
  2.5 0.2 multiply_convert_fusion
  2.7 0.1 fusion.22
  2.8 0.1 maximum_bitcast_fusion.2
  3.0 7.1 %fusion.3 = f32[4,48,2,1024]{3,1,0,2:T(8,128)S(1)} fusion(bf16[4,12,48,2,1024]{4,3,2,1,0:T(2,128)(2,1)} %param.7, bf16[12,48,1,2,48]{1,4,0,2,3:T(8,128)(2,1)S(1)} %get-tuple-element.8, bf16[12,48,1,2,48]{1,4,0,2,3:T(8,128)(2,1)S(1)} %get-tuple-element.7), kind=kOutput, calls=%fused_computation.3 | convolution fusion | flops 906412032 | bytes 11231232 | tf_op jit(solution)/shard_map/pncom,epncw->emow/dot_general | solution.py:96
  10.1 1.2 %copy.35 = f32[4,48,2,1024]{3,2,1,0:T(2,128)S(1)} copy(f32[4,48,2,1024]{3,1,0,2:T(8,128)S(1)} %fusion.3) | data formatting | bytes 3145728 | tf_op jit(solution)/shard_map/pncom,epncw->emow/transpose | solution.py:96
  11.4 0.1 dynamic-slice_bitcast_fusion
  11.4 0.0 copy-start
  11.4 0.1 collective-permute-start
  11.5 2.3 %collective-permute-done = f32[4,2,12,2,1024]{4,3,2,1,0:T(2,128)S(1)} collective-permute-done((f32[4,2,12,2,1024]{4,3,2,1,0:T(2,128)S(1)}, f32[4,2,12,2,1024]{4,3,2,1,0:T(2,128)S(1)}, u32[]{:S(2)}, u32[]{:S(2)}) %collective-permute-start) | collective-permute-done | bytes 786464 | tf_op jit(solution)/shard_map/ppermute | solution.py:100
  13.8 0.4 bitcast_add_fusion
  14.2 0.1 fusion.9
  14.4 0.9 collective-permute-start.1
  15.3 0.0 copy-done
  15.3 6.1 %collective-permute-done.1 = bf16[4,12,2,1024]{3,2,1,0:T(2,128)(2,1)S(1)} collective-permute-done((bf16[4,12,2,1024]{3,2,1,0:T(2,128)(2,1)S(1)}, bf16[4,12,2,1024]{3,2,1,0:T(2,128)(2,1)S(1)}, u32[]{:S(2)}, u32[]{:S(2)}) %collective-permute-start.1) | collective-permute-done | bytes 196640 | tf_op jit(solution)/shard_map/ppermute | solution.py:103
  21.4 0.2 fusion.8
  21.6 0.4 reshape.117
  22.0 0.0 copy-start.1
  22.0 0.3 copy.36
  22.3 0.4 reshape.118
  22.7 0.7 pad_maximum_fusion.1
  23.5 11.5 %all-to-all-start = ((bf16[32,30,128]{2,1,0:T(8,128)(2,1)}), bf16[32,30,128]{2,1,0:T(8,128)(2,1)S(1)}, u32[]{:S(2)}, u32[]{:S(2)}) async-start(bf16[32,30,128]{2,1,0:T(8,128)(2,1)} %pad_maximum_fusion.1), calls=%async_computation | async-start | bytes 524288 | tf_op jit(solution)/shard_map/all_to_all | solution.py:107
  35.0 0.0 copy-done.1
  35.0 0.1 copy.37
  35.2 0.6 pad.15.refs_1_
  35.8 11.5 %all-to-all-done = bf16[32,30,128]{2,1,0:T(8,128)(2,1)S(1)} async-done(((bf16[32,30,128]{2,1,0:T(8,128)(2,1)}), bf16[32,30,128]{2,1,0:T(8,128)(2,1)S(1)}, u32[]{:S(2)}, u32[]{:S(2)}) %all-to-all-start) | async-done | bytes 245792 | tf_op jit(solution)/shard_map/all_to_all | solution.py:107
  47.3 0.2 reshape.121
  47.5 1.5 %collective-permute-start.2 = (bf16[128,768]{1,0:T(8,128)(2,1)S(1)}, bf16[128,768]{1,0:T(8,128)(2,1)S(1)}, u32[]{:S(2)}, u32[]{:S(2)}) collective-permute-start(bf16[128,768]{1,0:T(8,128)(2,1)S(1)} %reshape.121), channel_id=1, source_target_pairs={{0,32},{32,0},{1,33},{33,1},{2,34},{34,2},{3,35},{35,3},{4,36},{36... | collective-permute-start | bytes 589832 | tf_op jit(solution)/shard_map/ppermute | solution.py:110
  49.1 0.6 fusion.13.refs_2_
  49.7 0.1 reshape.119
  49.7 0.7 pad.14.refs_0_
  50.4 4.4 %collective-permute-done.2 = bf16[128,768]{1,0:T(8,128)(2,1)S(1)} collective-permute-done((bf16[128,768]{1,0:T(8,128)(2,1)S(1)}, bf16[128,768]{1,0:T(8,128)(2,1)S(1)}, u32[]{:S(2)}, u32[]{:S(2)}) %collective-permute-start.2) | collective-permute-done | bytes 196640 | tf_op jit(solution)/shard_map/ppermute | solution.py:110
  54.8 0.8 pad_maximum_fusion.refs_3_
  55.6 28.9 %strengths.1 = f32[32,24,128]{2,1,0:T(8,128)} custom-call(bf16[8,8192]{1,0:T(8,128)(2,1)} %pad.14.refs_0_, bf16[256,8]{1,0:T(8,128)(2,1)} %pad.15.refs_1_, f32[8,128]{1,0:T(8,128)} %fusion.13.refs_2_, bf16[256,768]{1,0:T(8,128)(2,1)} %pad_maximum_fusion.refs_3_), custom_call_target="tpu_custom_call" | custom-call | flops 6442450944 | bytes 393216 | tf_op jit(solution)/shard_map/strengths/pallas_call | solution.py:63
  84.4 17.9 %all_to_all.10 = f32[32,24,128]{2,1,0:T(8,128)S(1)} all-to-all(f32[32,24,128]{2,1,0:T(8,128)} %strengths.1), channel_id=1, replica_groups=mesh['xl'=2,'core'=2,'xh'=2,'z'=8,'y'=4] {'z','y'}, dimensions={0} | all-to-all | bytes 786432 | tf_op jit(solution)/shard_map/all_to_all | solution.py:126
  102.3 0.1 copy.38
  102.4 0.8 copy.50
  (10 shorter events, 0.2 us)
Async XLA Ops:
  11.4 3.9 %copy-start = (s32[3,256]{1,0:T(4,128)S(1)}, s32[3,256]{1,0:T(4,128)}, u32[]{:S(2)}) copy-start(s32[3,256]{1,0:T(4,128)} %param.11) | copy-start | bytes 9220
  11.4 2.4 %collective-permute-start = (f32[4,2,12,2,1024]{4,3,2,1,0:T(2,128)S(1)}, f32[4,2,12,2,1024]{4,3,2,1,0:T(2,128)S(1)}, u32[]{:S(2)}, u32[]{:S(2)}) collective-permute-start(f32[4,2,12,2,1024]{4,3,2,1,0:T(2,128)S(1)} %dynamic-slice_bitcast_fusion), channel_id=1, source_target_pairs={{0,64},{64,0},{1,65},{65,1},{2,66},{66,2},{3,67},{67,3},{4,68},{68... | collective-permute-start | bytes 2359304 | tf_op jit(solution)/shard_map/ppermute | solution.py:100
  14.4 7.0 %collective-permute-start.1 = (bf16[4,12,2,1024]{3,2,1,0:T(2,128)(2,1)S(1)}, bf16[4,12,2,1024]{3,2,1,0:T(2,128)(2,1)S(1)}, u32[]{:S(2)}, u32[]{:S(2)}) collective-permute-start(bf16[4,12,2,1024]{3,2,1,0:T(2,128)(2,1)S(1)} %fusion.9), channel_id=1, source_target_pairs={{0,128},{128,0},{1,129},{129,1},{2,130},{130,2},{3,131},{131,3},{4... | collective-permute-start | bytes 589832 | tf_op jit(solution)/shard_map/ppermute | solution.py:103
  22.0 13.0 %copy-start.1 = (s32[3,256]{1,0:T(4,128)S(1)}, s32[3,256]{1,0:T(4,128)}, u32[]{:S(2)}) copy-start(s32[3,256]{1,0:T(4,128)} %param.8) | copy-start | bytes 9220
  23.5 23.8 %all-to-all-start = ((bf16[32,30,128]{2,1,0:T(8,128)(2,1)}), bf16[32,30,128]{2,1,0:T(8,128)(2,1)S(1)}, u32[]{:S(2)}, u32[]{:S(2)}) async-start(bf16[32,30,128]{2,1,0:T(8,128)(2,1)} %pad_maximum_fusion.1), calls=%async_computation | async-start | bytes 524288 | tf_op jit(solution)/shard_map/all_to_all | solution.py:107
  47.5 7.3 %collective-permute-start.2 = (bf16[128,768]{1,0:T(8,128)(2,1)S(1)}, bf16[128,768]{1,0:T(8,128)(2,1)S(1)}, u32[]{:S(2)}, u32[]{:S(2)}) collective-permute-start(bf16[128,768]{1,0:T(8,128)(2,1)S(1)} %reshape.121), channel_id=1, source_target_pairs={{0,32},{32,0},{1,33},{33,1},{2,34},{34,2},{3,35},{35,3},{4,36},{36... | collective-permute-start | bytes 589832 | tf_op jit(solution)/shard_map/ppermute | solution.py:110

commit v2 on v1

v2 whole, which is shorter than its diff:
```python
import math

import jax
import jax.numpy as jnp
from jax import lax
from jax.experimental import pallas as pl
from jax.experimental.pallas import tpu as pltpu
from jax.sharding import Mesh, PartitionSpec as P

W = 32
KGRID = 64
PH = ("xl", "core")
KA = ("xh", "z", "y")
SWAP = [(0, 1), (1, 0)]
CELLS = 128
K_STEP = 1024
K_BLOCK = 2048
EARLY = 6144
VMEM_MIB = 32


def coupling(q_angle, eigvec, omega):
    mode_scale = 1.0 / jnp.sqrt(2.0 * omega)
    cos_phase = jnp.cos(q_angle)[:, None, None]
    sin_phase = jnp.sin(q_angle)[:, None, None]
    real_part = eigvec[0][None]
    imag_part = eigvec[1][None]
    coef_re = ((cos_phase * real_part - sin_phase * imag_part) * mode_scale).astype(jnp.bfloat16)
    coef_im = ((sin_phase * real_part + cos_phase * imag_part) * mode_scale).astype(jnp.bfloat16)
    return jnp.stack([jnp.stack([coef_re, coef_im], 2), jnp.stack([-coef_im, coef_re], 2)], 2)


def fill_left(vert_ref, left, column):
    turned = vert_ref[...].astype(jnp.float32).T
    count = turned.shape[1]
    half = turned.shape[0] // 2
    left[:, column : column + count] = turned.astype(jnp.bfloat16)
    crossed = jnp.concatenate([-turned[half:], turned[:half]], 0)
    left[:, column + count : column + 2 * count] = crossed.astype(jnp.bfloat16)


def fill_phase(el_ref, kp_ref, trig_ref, phase, k_start, k_stop, run_start, run_stop):
    for k in range(k_start, k_stop, K_STEP):
        numer = lax.dot_general(
            el_ref[:, run_start * CELLS : run_stop * CELLS],
            kp_ref[:, k : k + K_STEP],
            (((0,), (0,)), ((), ())),
            preferred_element_type=jnp.float32,
        )
        index = numer.astype(jnp.int32) & 127
        for lane in range(0, K_STEP, 128):
            for run in range(numer.shape[0] // CELLS):
                part = index[run * CELLS : (run + 1) * CELLS, lane : lane + 128]
                for which in range(2):
                    values = jnp.broadcast_to(trig_ref[which : which + 1, :], part.shape)
                    found = jnp.take_along_axis(values, part, axis=1)
                    row = (2 * (run_start + run) + which) * CELLS
                    phase[row : row + CELLS, k + lane : k + lane + 128] = found.astype(jnp.bfloat16)


def own_kernel(vert_ref, kp_ref, el_ref, trig_ref, out_ref, left, phase):
    fill_left(vert_ref, left, 0)
    early = out_ref.shape[1]
    fill_phase(el_ref, kp_ref, trig_ref, phase, 0, early, 0, 1)
    for k in range(0, early, K_BLOCK):
        part = phase[: 2 * CELLS, k : k + K_BLOCK]
        out_ref[:, k : k + K_BLOCK] = jnp.dot(left[...], part, preferred_element_type=jnp.float32)


def strength_kernel(
    modes, scale, own_ref, other_ref, kp_ref, el_ref, trig_ref, sum_ref, out_ref, left, phase
):
    fill_left(own_ref, left, 0)
    fill_left(other_ref, left, 2 * CELLS)
    k_count = kp_ref.shape[1]
    early = sum_ref.shape[1]
    width = k_count // out_ref.shape[0]
    fill_phase(el_ref, kp_ref, trig_ref, phase, 0, early, 1, 2)
    fill_phase(el_ref, kp_ref, trig_ref, phase, early, k_count, 0, 2)
    for k in range(0, k_count, K_BLOCK):
        at = slice(k, k + K_BLOCK)
        if k < early:
            bloch = sum_ref[:, at] + jnp.dot(
                left[:, 2 * CELLS :], phase[2 * CELLS :, at], preferred_element_type=jnp.float32
            )
        else:
            bloch = jnp.dot(left[...], phase[:, at], preferred_element_type=jnp.float32)
        square = (bloch * bloch).reshape(2 * modes, W, K_BLOCK)
        total = jnp.sum(square[:modes] + square[modes:], axis=1) * scale
        for lane in range(0, K_BLOCK, 128):
            dest, row = divmod(k + lane, width)
            row = row // 128 * modes
            out_ref[dest, row : row + modes, :] = total[:, lane : lane + 128]


def strengths(own, other, kp, el, trig, modes, scale, dests):
    cells, cols = own.shape
    k_count = kp.shape[1]
    early = EARLY
    vmem = pl.BlockSpec(memory_space=pltpu.VMEM)
    params = pltpu.CompilerParams(vmem_limit_bytes=VMEM_MIB * 2**20)
    f32, bf16 = jnp.float32, jnp.bfloat16
    summed = pl.pallas_call(
        own_kernel,
        out_shape=pltpu.VMEM((cols, early), f32),
        in_specs=[vmem] * 4,
        out_specs=vmem,
        scratch_shapes=[
            pltpu.VMEM((cols, 2 * cells), bf16),
            pltpu.VMEM((2 * cells, early), bf16),
        ],
        compiler_params=params,
        cost_estimate=pl.CostEstimate(
            flops=4 * cols * cells * early, bytes_accessed=4 * cols * early, transcendentals=0
        ),
        name="own",
    )(own, kp, el, trig)
    return pl.pallas_call(
        lambda *refs: strength_kernel(modes, scale, *refs),
        out_shape=jax.ShapeDtypeStruct((dests, modes * k_count // dests // 128, 128), f32),
        in_specs=[vmem] * 6,
        out_specs=vmem,
        scratch_shapes=[
            pltpu.VMEM((cols, 4 * cells), bf16),
            pltpu.VMEM((4 * cells, k_count), bf16),
        ],
        compiler_params=params,
        cost_estimate=pl.CostEstimate(
            flops=8 * cols * cells * k_count, bytes_accessed=4 * cols * early, transcendentals=0
        ),
        name="strengths",
    )(own, other, kp, el, trig, summed)


def shards(g_wan, el_cells, ph_cells, q_point, kpoints, eigvec, omega):
    bf16, f32 = jnp.bfloat16, jnp.float32
    xl, core, xh = (lax.axis_index(a) for a in ("xl", "core", "xh"))
    e = g_wan.shape[0]
    k_dev = kpoints.shape[1]
    nu = eigvec.shape[1]
    modes = nu // 4
    unit = 2.0 * math.pi / KGRID
    q_sum = jnp.sum(q_point[:, None] * ph_cells, axis=0)
    q_angle = jnp.mod(q_sum, KGRID).astype(f32) * unit

    def reorder(x):
        lead = x.shape[:-1]
        return x.reshape(*lead, 2, 2, modes).swapaxes(-3, -2).reshape(*lead, nu)

    table = coupling(q_angle, reorder(eigvec), reorder(omega))
    partial = jnp.einsum("pncom,epncw->oemw", table, g_wan, preferred_element_type=f32)
    mine = lax.dynamic_slice_in_dim(partial, core * 2 * modes, 2 * modes, 2)
    theirs = lax.dynamic_slice_in_dim(partial, (1 - core) * 2 * modes, 2 * modes, 2)
    both = mine + lax.ppermute(theirs, "core", SWAP)
    mine = lax.dynamic_slice_in_dim(both, xl * modes, modes, 2)
    theirs = lax.dynamic_slice_in_dim(both, (1 - xl) * modes, modes, 2).astype(bf16)
    mine, theirs = mine.reshape(-1, W * W), theirs.reshape(-1, W * W)
    vert = (mine + lax.ppermute(theirs, "xl", SWAP).astype(f32)).astype(bf16)
    vert = vert.reshape(2, e, modes, W, W).transpose(3, 1, 0, 2, 4).reshape(W, -1, 128)
    kp = jnp.broadcast_to(kpoints.astype(bf16).reshape(1, -1, 128), (W, 3 * k_dev // 128, 128))
    rows = vert.shape[1]
    moved = lax.all_to_all(jnp.concatenate([vert, kp], 1), ("z", "y"), 0, 0, tiled=True)
    own = moved[:, :rows].reshape(W * e, 2 * modes * W)
    kp = moved[:, rows:].reshape(W, 3, k_dev).transpose(1, 0, 2).reshape(3, W * k_dev)
    other = lax.ppermute(own, "xh", SWAP)
    half = W * e
    el = el_cells.astype(bf16)
    el = jnp.concatenate(
        [
            lax.dynamic_slice_in_dim(el, xh * half, half, 1),
            lax.dynamic_slice_in_dim(el, (1 - xh) * half, half, 1),
        ],
        1,
    )
    el = jnp.pad(el, ((0, 5), (0, 0)))
    kp = jnp.pad(kp, ((0, 5), (0, 0)))
    angle = (jnp.arange(128) % KGRID).astype(f32) * unit
    trig = jnp.stack([jnp.cos(angle), jnp.sin(angle)]).astype(bf16).astype(f32)
    trig = jnp.pad(trig, ((0, 6), (0, 0)))
    scale = 1.0 / float(el_cells.shape[1] * nu * W)
    found = strengths(own, other, kp, el, trig, modes, scale, W)
    found = lax.all_to_all(found, ("z", "y"), 0, 0, tiled=True)
    found = found.reshape(W, k_dev // 128, modes, 128).transpose(2, 0, 1, 3)
    return found.reshape(modes, W, k_dev)


def solution(mesh):
    split = Mesh(mesh.devices.reshape(2, 2, 2, 8, 4), PH + KA)
    return jax.shard_map(
        shards,
        mesh=split,
        in_specs=(
            P(KA, PH, None, None, None),
            P(),
            P(None, PH),
            P(),
            P(None, KA),
            P(),
            P(),
        ),
        out_specs=P(PH, None, KA),
        check_vma=False,
    )
```

time: 104 us -> 79.9 us (0.77)
  Pallas kernels: 28.9 us -> 10.5 us
  local copies, waits for them, and re-layouts: 6.06 us -> 4.19 us
  other arithmetic: 4.79 us -> 2.96 us
  waiting for transfers between devices: 24.2 us -> 22.6 us
    pallas_call x1 -> x2, Pallas kernels: 28.9 us -> 10.5 us  [the longest x1 6.99 us: strengths(): pl.pallas_call(lambda *refs: strength_kernel(modes, scale, *refs), out_sh...]
    ppermute x1, waiting for transfers between devices: 4.38 us -> 2.19 us  [shards(): other = lax.ppermute(own, 'xh', SWAP)]
    transpose x2 -> x0, local copies, waits for them, and re-layouts: 1.52 us -> none  [the longest x1 1.22 us: shards(): jnp.einsum('pncom,epncw->emow', table, g_wan, preferred_element_type=f32)]
  transfers between devices with their start and end apart: 4 -> 4, of which waited for: 4 -> 4; matrix products, arithmetic and copies ran while one was open for 2% -> 0% of each run, Pallas kernels for 0% -> 4%
where the time goes in v2:
time: 79.9 us; the launch traced here: 79.6 us
  waiting for transfers between devices  22.6 us (28%)
  blocking collectives  17.7 us (22%)
  starting transfers between devices  14.2 us (18%)
  Pallas kernels  10.5 us (13%)
  matrix products  7.15 us (9%)
  local copies, waits for them, and re-layouts  4.19 us (5%)
  other arithmetic  2.96 us (4%)
    all_to_all x1, blocking collectives, shards(): found = lax.all_to_all(found, ('z', 'y'), 0, 0, tiled=True)  17.7 us
    all_to_all x1, waiting for transfers between devices, shards(): lax.all_to_all(jnp.concatenate([vert, kp], 1), ('z', 'y'), 0, 0, tiled=True)  12.2 us
    all_to_all x1, starting transfers between devices, shards(): lax.all_to_all(jnp.concatenate([vert, kp], 1), ('z', 'y'), 0, 0, tiled=True)  11.5 us
    dot_general x1, matrix products, shards(): jnp.einsum('pncom,epncw->oemw', table, g_wan, preferred_element_type=f32)  7.15 us
    pallas_call x1, Pallas kernels, strengths(): pl.pallas_call(lambda *refs: strength_kernel(modes, scale, *refs), out_sh...  6.99 us
    ppermute x1, waiting for transfers between devices, shards(): vert = (mine + lax.ppermute(theirs, 'xl', SWAP).astype(f32)).astype(bf16)  5.95 us
    pallas_call x1, Pallas kernels, strengths(): pl.pallas_call(own_kernel, out_shape=pltpu.VMEM((cols, early), f32), in_s...  3.56 us
    ppermute x1, waiting for transfers between devices, shards(): both = mine + lax.ppermute(theirs, 'core', SWAP)  2.25 us
  transfers between devices with their start and end apart: 4, of which 4 were waited for; matrix products, arithmetic and copies ran while one was open for 0% of the time, Pallas kernels for 4%

profile of v2, /device:TPU:6, one launch (start us, length us, event | category | flops | bytes accessed | tf_op | source)
XLA Modules:
  0.0 79.6 jit_solution(4922338296582138857)
XLA Ops:
  0.0 0.7 multiply_rsqrt_fusion
  0.7 0.8 multiply_reduce_fusion
  1.4 0.1 fusion.22
  1.5 0.1 sqrt.10
  1.6 0.1 sqrt.12
  1.7 0.9 %copy.23 = f32[2,48,48]{1,0,2:T(2,128)S(1)} copy(f32[2,48,48]{2,1,0:T(8,128)} %param.12) | data formatting | bytes 36864 | tf_op args[5]
  2.7 0.1 fusion.21
  2.8 0.2 multiply_convert_fusion
  3.1 0.1 maximum_bitcast_fusion.2
  3.2 7.1 %fusion.3 = f32[2,48,4,1024]{3,1,2,0:T(8,128)S(1)} fusion(bf16[4,12,48,2,1024]{4,3,2,1,0:T(2,128)(2,1)} %param.7, bf16[12,48,1,2,48]{1,4,0,2,3:T(8,128)(2,1)S(1)} %get-tuple-element.8, bf16[12,48,1,2,48]{1,4,0,2,3:T(8,128)(2,1)S(1)} %get-tuple-element.7), kind=kOutput, calls=%fused_computation.3 | convolution fusion | flops 906412032 | bytes 11231232 | tf_op jit(solution)/shard_map/pncom,epncw->oemw/dot_general | solution.py:151
  10.4 0.1 dynamic-slice_bitcast_fusion
  10.5 0.1 collective-permute-start
  10.6 0.0 copy-start
  10.6 2.2 %collective-permute-done = f32[2,4,24,1024]{3,2,1,0:T(8,128)S(1)} collective-permute-done((f32[2,4,24,1024]{3,2,1,0:T(8,128)S(1)}, f32[2,4,24,1024]{3,2,1,0:T(8,128)S(1)}, u32[]{:S(2)}, u32[]{:S(2)}) %collective-permute-start) | collective-permute-done | bytes 786464 | tf_op jit(solution)/shard_map/ppermute | solution.py:154
  12.8 0.1 bitcast_add_fusion
  13.0 0.1 dynamic-slice_convert_fusion
  13.1 0.9 %collective-permute-start.1 = (bf16[96,1024]{1,0:T(8,128)(2,1)S(1)}, bf16[96,1024]{1,0:T(8,128)(2,1)S(1)}, u32[]{:S(2)}, u32[]{:S(2)}) collective-permute-start(bf16[96,1024]{1,0:T(8,128)(2,1)S(1)} %reshape.141), channel_id=1, source_target_pairs={{0,128},{128,0},{1,129},{129,1},{2,130},{130,2},{3,131},{131,3},{4... | collective-permute-start | bytes 589832 | tf_op jit(solution)/shard_map/ppermute | solution.py:158
  14.0 0.0 copy-done
  14.0 0.1 constant_dynamic-slice_fusion.2
  14.2 6.0 %collective-permute-done.1 = bf16[96,1024]{1,0:T(8,128)(2,1)S(1)} collective-permute-done((bf16[96,1024]{1,0:T(8,128)(2,1)S(1)}, bf16[96,1024]{1,0:T(8,128)(2,1)S(1)}, u32[]{:S(2)}, u32[]{:S(2)}) %collective-permute-start.1) | collective-permute-done | bytes 196640 | tf_op jit(solution)/shard_map/ppermute | solution.py:158
  20.2 0.6 reshape.142
  20.7 0.3 copy.43
  21.1 0.0 copy-start.1
  21.1 0.6 reshape.143
  21.7 0.7 pad_maximum_fusion
  22.5 11.5 %all-to-all-start = ((bf16[32,30,128]{2,1,0:T(8,128)(2,1)}), bf16[32,30,128]{2,1,0:T(8,128)(2,1)S(1)}, u32[]{:S(2)}, u32[]{:S(2)}) async-start(bf16[32,30,128]{2,1,0:T(8,128)(2,1)} %pad_maximum_fusion), calls=%async_computation | async-start | bytes 524288 | tf_op jit(solution)/shard_map/all_to_all | solution.py:162
  34.0 0.0 copy-done.1
  34.1 12.2 %all-to-all-done = bf16[32,30,128]{2,1,0:T(8,128)(2,1)S(1)} async-done(((bf16[32,30,128]{2,1,0:T(8,128)(2,1)}), bf16[32,30,128]{2,1,0:T(8,128)(2,1)S(1)}, u32[]{:S(2)}, u32[]{:S(2)}) %all-to-all-start) | async-done | bytes 245792 | tf_op jit(solution)/shard_map/all_to_all | solution.py:162
  46.3 0.2 reshape.144.vert_ref.refs_0_
  46.5 0.1 reshape.145
  46.6 1.7 %collective-permute-start.2 = (bf16[128,768]{1,0:T(8,128)(2,1)S(1)}, bf16[128,768]{1,0:T(8,128)(2,1)S(1)}, u32[]{:S(2)}, u32[]{:S(2)}) collective-permute-start(bf16[128,768]{1,0:T(8,128)(2,1)S(1)} %reshape.144.vert_ref.refs_0_), channel_id=1, source_target_pairs={{0,32},{32,0},{1,33},{33,1},{2,34},{34,2},{3,35},{35,3},{4,36},{36... | collective-permute-start | bytes 589832 | tf_op jit(solution)/shard_map/ppermute | solution.py:165
  48.3 3.6 %own.1.refs_5_ = f32[768,6144]{1,0:T(8,128)S(1)} custom-call(bf16[128,768]{1,0:T(8,128)(2,1)S(1)} %reshape.144.vert_ref.refs_0_, bf16[8,8192]{1,0:T(8,128)(2,1)S(1)} %pad.14.kp_ref.refs_2_, bf16[8,256]{1,0:T(8,128)(2,1)S(1)} %fusion.10.el_ref.refs_3_, f32[8,128]{1,0:T(8,128)S(1)} %fusion.14.trig_ref.refs_4_), custom_call_target="tpu_custom_call" | custom-call | flops 2415919104 | bytes 18874368 | tf_op jit(solution)/shard_map/own/pallas_call | solution.py:103
  51.9 2.2 %collective-permute-done.2.refs_1_ = bf16[128,768]{1,0:T(8,128)(2,1)S(1)} collective-permute-done((bf16[128,768]{1,0:T(8,128)(2,1)S(1)}, bf16[128,768]{1,0:T(8,128)(2,1)S(1)}, u32[]{:S(2)}, u32[]{:S(2)}) %collective-permute-start.2) | collective-permute-done | bytes 196640 | tf_op jit(solution)/shard_map/ppermute | solution.py:165
  54.0 7.0 %strengths.1 = f32[32,24,128]{2,1,0:T(8,128)S(1)} custom-call(bf16[128,768]{1,0:T(8,128)(2,1)S(1)} %reshape.144.vert_ref.refs_0_, bf16[128,768]{1,0:T(8,128)(2,1)S(1)} %collective-permute-done.2.refs_1_, bf16[8,8192]{1,0:T(8,128)(2,1)S(1)} %pad.14.kp_ref.refs_2_, bf16[8,256]{1,0:T(8,128)(2,1)S(1)} %fusion.10.el_ref.refs_3_, ...), custom_call_target="tpu_custom_call" | custom-call | flops 6442450944 | bytes 18874368 | tf_op jit(solution)/shard_map/strengths/pallas_call | solution.py:118
  61.0 17.7 %all_to_all.10 = f32[32,24,128]{2,1,0:T(8,128)S(1)} all-to-all(f32[32,24,128]{2,1,0:T(8,128)S(1)} %strengths.1), channel_id=1, replica_groups=mesh['xl'=2,'core'=2,'xh'=2,'z'=8,'y'=4] {'z','y'}, dimensions={0} | all-to-all | bytes 786432 | tf_op jit(solution)/shard_map/all_to_all | solution.py:182
  78.7 0.1 copy.30
  78.8 0.8 copy.44
  (21 shorter events, 0.4 us)
Async XLA Ops:
  10.5 2.4 %collective-permute-start = (f32[2,4,24,1024]{3,2,1,0:T(8,128)S(1)}, f32[2,4,24,1024]{3,2,1,0:T(8,128)S(1)}, u32[]{:S(2)}, u32[]{:S(2)}) collective-permute-start(f32[2,4,24,1024]{3,2,1,0:T(8,128)S(1)} %dynamic-slice_bitcast_fusion), channel_id=1, source_target_pairs={{0,64},{64,0},{1,65},{65,1},{2,66},{66,2},{3,67},{67,3},{4,68},{68... | collective-permute-start | bytes 2359304 | tf_op jit(solution)/shard_map/ppermute | solution.py:154
  10.6 3.4 %copy-start = (s32[3,256]{1,0:T(4,128)S(1)}, s32[3,256]{1,0:T(4,128)}, u32[]{:S(2)}) copy-start(s32[3,256]{1,0:T(4,128)} %param.11) | copy-start | bytes 9220
  13.1 7.0 %collective-permute-start.1 = (bf16[96,1024]{1,0:T(8,128)(2,1)S(1)}, bf16[96,1024]{1,0:T(8,128)(2,1)S(1)}, u32[]{:S(2)}, u32[]{:S(2)}) collective-permute-start(bf16[96,1024]{1,0:T(8,128)(2,1)S(1)} %reshape.141), channel_id=1, source_target_pairs={{0,128},{128,0},{1,129},{129,1},{2,130},{130,2},{3,131},{131,3},{4... | collective-permute-start | bytes 589832 | tf_op jit(solution)/shard_map/ppermute | solution.py:158
  21.1 12.9 %copy-start.1 = (s32[3,256]{1,0:T(4,128)S(1)}, s32[3,256]{1,0:T(4,128)}, u32[]{:S(2)}) copy-start(s32[3,256]{1,0:T(4,128)} %param.8) | copy-start | bytes 9220
  22.5 23.8 %all-to-all-start = ((bf16[32,30,128]{2,1,0:T(8,128)(2,1)}), bf16[32,30,128]{2,1,0:T(8,128)(2,1)S(1)}, u32[]{:S(2)}, u32[]{:S(2)}) async-start(bf16[32,30,128]{2,1,0:T(8,128)(2,1)} %pad_maximum_fusion), calls=%async_computation | async-start | bytes 524288 | tf_op jit(solution)/shard_map/all_to_all | solution.py:162
  46.6 7.4 %collective-permute-start.2 = (bf16[128,768]{1,0:T(8,128)(2,1)S(1)}, bf16[128,768]{1,0:T(8,128)(2,1)S(1)}, u32[]{:S(2)}, u32[]{:S(2)}) collective-permute-start(bf16[128,768]{1,0:T(8,128)(2,1)S(1)} %reshape.144.vert_ref.refs_0_), channel_id=1, source_target_pairs={{0,32},{32,0},{1,33},{33,1},{2,34},{34,2},{3,35},{35,3},{4,36},{36... | collective-permute-start | bytes 589832 | tf_op jit(solution)/shard_map/ppermute | solution.py:165

commit v3 on v2

--- a/solution.py
+++ b/solution.py
@@ -2,6 +2,7 @@
 
 import jax
 import jax.numpy as jnp
+import numpy as np
 from jax import lax
 from jax.experimental import pallas as pl
 from jax.experimental.pallas import tpu as pltpu
@@ -17,17 +18,135 @@
 K_BLOCK = 2048
 EARLY = 6144
 VMEM_MIB = 32
-
-
-def coupling(q_angle, eigvec, omega):
-    mode_scale = 1.0 / jnp.sqrt(2.0 * omega)
-    cos_phase = jnp.cos(q_angle)[:, None, None]
-    sin_phase = jnp.sin(q_angle)[:, None, None]
-    real_part = eigvec[0][None]
-    imag_part = eigvec[1][None]
-    coef_re = ((cos_phase * real_part - sin_phase * imag_part) * mode_scale).astype(jnp.bfloat16)
-    coef_im = ((sin_phase * real_part + cos_phase * imag_part) * mode_scale).astype(jnp.bfloat16)
-    return jnp.stack([jnp.stack([coef_re, coef_im], 2), jnp.stack([-coef_im, coef_re], 2)], 2)
+TRIO = 3
+SENT = jnp.float16
+ROOT_SCALE = 64.0
+
+
+def row_table():
+    rows = np.arange(2 * 2 * 4 * 2 * TRIO)
+    trio, rest = rows % TRIO, rows // TRIO
+    part, rest = rest % 2, rest // 2
+    group, rest = rest % 4, rest // 4
+    table = np.zeros((rows.size, 8), np.int32)
+    table[:, 0] = group * TRIO + trio
+    table[:, 1] = part
+    table[:, 2] = rest % 2
+    table[:, 3] = rest // 2
+    return table
+
+
+def trig_table(count):
+    unit = np.float32(2.0 * math.pi / KGRID)
+    angle = (np.arange(count) % KGRID).astype(np.float32) * unit
+    return np.stack([np.cos(angle), np.sin(angle)]).astype(np.float32)
+
+
+def fill_coupling(q_ref, cells_ref, trig_ref, eig_ref, omega_ref, rows_ref, table):
+    nu = omega_ref.shape[1]
+    count = rows_ref.shape[0]
+    modes = nu // 4
+    core, xl = lax.axis_index("core"), lax.axis_index("xl")
+    at_core = jnp.where(rows_ref[:, 3:4] == 1, core, 1 - core)
+    at_xl = jnp.where(rows_ref[:, 2:3] == 1, xl, 1 - xl)
+    mode = rows_ref[:, 0:1] + (2 * at_xl + at_core) * modes
+    pick = (lax.broadcasted_iota(jnp.int32, (count, nu), 1) == mode).astype(jnp.float32)
+    inverse = 1.0 / jnp.sqrt(2.0 * omega_ref[...])
+    scale = jnp.sum(pick * inverse, axis=1, keepdims=True)
+    column = lax.broadcasted_iota(jnp.int32, (nu, 2 * nu), 1)
+    twice = lax.broadcasted_iota(jnp.int32, (nu, 2 * nu), 0)
+    spread = ((column == 2 * twice) | (column == 2 * twice + 1)).astype(jnp.float32)
+    high = lax.Precision.HIGHEST
+    planes = []
+    for part in range(2):
+        picked = lax.dot_general(
+            pick, eig_ref[part], (((1,), (1,)), ((), ())),
+            precision=high, preferred_element_type=jnp.float32,
+        )
+        planes.append(
+            jnp.dot(picked, spread, precision=high, preferred_element_type=jnp.float32)
+        )
+    re, im = planes
+    odd = (lax.broadcasted_iota(jnp.int32, (count, 2 * nu), 1) & 1) == 1
+    lower = jnp.broadcast_to(rows_ref[:, 1:2], (count, 2 * nu)) == 1
+    of_cos = jnp.where(lower, jnp.where(odd, re, im), jnp.where(odd, -im, re))
+    of_sin = jnp.where(lower, jnp.where(odd, -im, re), jnp.where(odd, -re, -im))
+    for p in range(cells_ref.shape[1]):
+        turn = sum(q_ref[d] * cells_ref[d, p] for d in range(3)) & (KGRID - 1)
+        value = (trig_ref[0, turn] * of_cos + trig_ref[1, turn] * of_sin) * scale
+        table[:, p * 2 * nu : (p + 1) * 2 * nu] = value.astype(jnp.bfloat16)
+
+
+def vertex_kernel(
+    q_hbm, cells_hbm, trig_hbm, eig_hbm, omega_hbm, rows_hbm, g_ref, theirs_ref, mine_ref,
+    q_ref, cells_ref, trig_ref, eig_ref, omega_ref, rows_ref, held, flat, table, small, sems,
+):
+    e_count, p_count, nu = g_ref.shape[:3]
+    sources = (q_hbm, cells_hbm, trig_hbm, eig_hbm, omega_hbm, rows_hbm)
+    targets = (q_ref, cells_ref, trig_ref, eig_ref, omega_ref, rows_ref)
+    first = [
+        pltpu.make_async_copy(source, target, small.at[i])
+        for i, (source, target) in enumerate(zip(sources, targets))
+    ]
+    copies = [pltpu.make_async_copy(g_ref.at[e], held.at[e], sems.at[e]) for e in range(e_count)]
+    for copy in first + copies:
+        copy.start()
+    for copy in first:
+        copy.wait()
+    fill_coupling(q_ref, cells_ref, trig_ref, eig_ref, omega_ref, rows_ref, table)
+    part = 2 * TRIO
+
+    def flatten(e):
+        copies[e].wait()
+        for p in range(p_count):
+            flat[e % 2, p * 2 * nu : (p + 1) * 2 * nu, :] = held[e, p].reshape(2 * nu, W * W)
+
+    flatten(0)
+    for e in range(e_count):
+        if e + 1 < e_count:
+            flatten(e + 1)
+        found = jnp.dot(table[...], flat[e % 2], preferred_element_type=jnp.float32)
+        row = 0
+        for out_ref in (theirs_ref, mine_ref):
+            for side in range(2):
+                for group in range(4):
+                    to = (group * e_count + e) * part
+                    out_ref[side, to : to + part, :] = found[row : row + part]
+                    row += part
+
+
+def partial_vertices(q_point, ph_cells, eigvec, omega, g_wan):
+    e, p, nu = g_wan.shape[:3]
+    rows = row_table()
+    out = pltpu.VMEM((2, e * rows.shape[0] // 4, W * W), jnp.float32)
+    vmem = pl.BlockSpec(memory_space=pltpu.VMEM)
+    hbm = pl.BlockSpec(memory_space=pltpu.HBM)
+    taken = [q_point, ph_cells, trig_table(KGRID), eigvec, omega.reshape(1, nu), rows, g_wan]
+    taken = [pltpu.with_memory_space_constraint(jnp.asarray(x), pltpu.HBM) for x in taken]
+    return pl.pallas_call(
+        vertex_kernel,
+        out_shape=(out, out),
+        in_specs=[hbm] * 7,
+        out_specs=(vmem, vmem),
+        scratch_shapes=[
+            pltpu.SMEM(q_point.shape, jnp.int32),
+            pltpu.SMEM(ph_cells.shape, jnp.int32),
+            pltpu.SMEM((2, KGRID), jnp.float32),
+            pltpu.VMEM(eigvec.shape, jnp.float32),
+            pltpu.VMEM((1, nu), jnp.float32),
+            pltpu.VMEM(rows.shape, jnp.int32),
+            pltpu.VMEM(g_wan.shape, g_wan.dtype),
+            pltpu.VMEM((2, p * 2 * nu, W * W), jnp.bfloat16),
+            pltpu.VMEM((rows.shape[0], p * 2 * nu), jnp.bfloat16),
+            pltpu.SemaphoreType.DMA((6,)),
+            pltpu.SemaphoreType.DMA((e,)),
+        ],
+        compiler_params=pltpu.CompilerParams(vmem_limit_bytes=40 * 2**20),
+        cost_estimate=pl.CostEstimate(
+            flops=2 * rows.shape[0] * g_wan.size, bytes_accessed=2 * g_wan.size, transcendentals=0
+        ),
+        name="vertices",
+    )(*taken)
 
 
 def fill_left(vert_ref, left, column):
@@ -132,34 +251,72 @@
     )(own, other, kp, el, trig, summed)
 
 
+def pack_kernel(mine_ref, core_ref, passed_ref, kp_ref, out_ref):
+    lanes = kp_ref.shape[1]
+    halves = [slice(lane, lane + 128) for lane in range(0, lanes, 128)]
+    kp = jnp.concatenate([kp_ref[d : d + 1, at] for d in range(3) for at in halves])
+    kp = kp.astype(jnp.float32).astype(jnp.bfloat16)
+    rows = out_ref.shape[1] - kp.shape[0]
+    total = mine_ref[1] + core_ref[1] + passed_ref[...].astype(jnp.float32)
+    total = total.astype(jnp.bfloat16)
+    for block in range(out_ref.shape[0]):
+        lane, group = block // 4 * 128, block % 4 * rows
+        out_ref[block, :rows, :] = total[group : group + rows, lane : lane + 128]
+        out_ref[block, rows:, :] = kp
+
+
+def pack(mine, core_part, passed, kp):
+    rows = passed.shape[0] // 4 + kp.size // 128
+    vmem = pl.BlockSpec(memory_space=pltpu.VMEM)
+    return pl.pallas_call(
+        pack_kernel,
+        out_shape=jax.ShapeDtypeStruct((W, rows, 128), jnp.bfloat16),
+        in_specs=[vmem] * 4,
+        out_specs=vmem,
+        compiler_params=pltpu.CompilerParams(vmem_limit_bytes=16 * 2**20),
+        name="pack",
+    )(mine, core_part, passed, kp)
+
+
+def unpack_kernel(in_ref, out_ref):
+    halves = out_ref.shape[2] // 128
+    for block in range(in_ref.shape[0]):
+        root = in_ref[block] * (1.0 / ROOT_SCALE)
+        square = root * root
+        value = square * square
+        first, group = block // 4 * 4, block % 4 * TRIO
+        for half in range(halves):
+            for trio in range(TRIO):
+                row = (half * TRIO + trio) * 4
+                lanes = slice(half * 128, half * 128 + 128)
+                out_ref[group + trio, first : first + 4, lanes] = value[row : row + 4]
+
+
+def unpack(found, modes, k_dev):
+    vmem = pl.BlockSpec(memory_space=pltpu.VMEM)
+    return pl.pallas_call(
+        unpack_kernel,
+        out_shape=jax.ShapeDtypeStruct((modes, W, k_dev), jnp.float32),
+        in_specs=[vmem],
+        out_specs=vmem,
+        compiler_params=pltpu.CompilerParams(vmem_limit_bytes=16 * 2**20),
+        name="unpack",
+    )(found)
+
+
 def shards(g_wan, el_cells, ph_cells, q_point, kpoints, eigvec, omega):
     bf16, f32 = jnp.bfloat16, jnp.float32
-    xl, core, xh = (lax.axis_index(a) for a in ("xl", "core", "xh"))
+    xh = lax.axis_index("xh")
     e = g_wan.shape[0]
     k_dev = kpoints.shape[1]
     nu = eigvec.shape[1]
     modes = nu // 4
-    unit = 2.0 * math.pi / KGRID
-    q_sum = jnp.sum(q_point[:, None] * ph_cells, axis=0)
-    q_angle = jnp.mod(q_sum, KGRID).astype(f32) * unit
-
-    def reorder(x):
-        lead = x.shape[:-1]
-        return x.reshape(*lead, 2, 2, modes).swapaxes(-3, -2).reshape(*lead, nu)
-
-    table = coupling(q_angle, reorder(eigvec), reorder(omega))
-    partial = jnp.einsum("pncom,epncw->oemw", table, g_wan, preferred_element_type=f32)
-    mine = lax.dynamic_slice_in_dim(partial, core * 2 * modes, 2 * modes, 2)
-    theirs = lax.dynamic_slice_in_dim(partial, (1 - core) * 2 * modes, 2 * modes, 2)
-    both = mine + lax.ppermute(theirs, "core", SWAP)
-    mine = lax.dynamic_slice_in_dim(both, xl * modes, modes, 2)
-    theirs = lax.dynamic_slice_in_dim(both, (1 - xl) * modes, modes, 2).astype(bf16)
-    mine, theirs = mine.reshape(-1, W * W), theirs.reshape(-1, W * W)
-    vert = (mine + lax.ppermute(theirs, "xl", SWAP).astype(f32)).astype(bf16)
-    vert = vert.reshape(2, e, modes, W, W).transpose(3, 1, 0, 2, 4).reshape(W, -1, 128)
-    kp = jnp.broadcast_to(kpoints.astype(bf16).reshape(1, -1, 128), (W, 3 * k_dev // 128, 128))
-    rows = vert.shape[1]
-    moved = lax.all_to_all(jnp.concatenate([vert, kp], 1), ("z", "y"), 0, 0, tiled=True)
+    theirs, mine = partial_vertices(q_point, ph_cells, eigvec, omega, g_wan)
+    core_part = lax.ppermute(theirs, "core", SWAP)
+    passed = lax.ppermute((mine[0] + core_part[0]).astype(bf16), "xl", SWAP)
+    sent = pack(mine, core_part, passed, kpoints)
+    rows = passed.shape[0] // 4
+    moved = lax.all_to_all(sent, ("z", "y"), 0, 0, tiled=True)
     own = moved[:, :rows].reshape(W * e, 2 * modes * W)
     kp = moved[:, rows:].reshape(W, 3, k_dev).transpose(1, 0, 2).reshape(3, W * k_dev)
     other = lax.ppermute(own, "xh", SWAP)
@@ -174,14 +331,12 @@
     )
     el = jnp.pad(el, ((0, 5), (0, 0)))
     kp = jnp.pad(kp, ((0, 5), (0, 0)))
-    angle = (jnp.arange(128) % KGRID).astype(f32) * unit
-    trig = jnp.stack([jnp.cos(angle), jnp.sin(angle)]).astype(bf16).astype(f32)
-    trig = jnp.pad(trig, ((0, 6), (0, 0)))
+    trig = np.pad(trig_table(128), ((0, 6), (0, 0)))
     scale = 1.0 / float(el_cells.shape[1] * nu * W)
     found = strengths(own, other, kp, el, trig, modes, scale, W)
-    found = lax.all_to_all(found, ("z", "y"), 0, 0, tiled=True)
-    found = found.reshape(W, k_dev // 128, modes, 128).transpose(2, 0, 1, 3)
-    return found.reshape(modes, W, k_dev)
+    root = jnp.sqrt(jnp.sqrt(found)) * ROOT_SCALE
+    found = lax.all_to_all(root.astype(SENT), ("z", "y"), 0, 0, tiled=True)
+    return unpack(found.astype(f32), modes, k_dev)
 
 
 def solution(mesh):

time: 79.9 us -> 73.1 us (0.915)
  Pallas kernels: 10.5 us -> 19.5 us
  matrix products: 7.15 us -> 0 us
  blocking collectives: 17.7 us -> 14.8 us
  local copies, waits for them, and re-layouts: 4.19 us -> 1.67 us
  other arithmetic: 2.96 us -> 1 us
  waiting for transfers between devices: 22.6 us -> 21.5 us
    pallas_call x0 -> x3, Pallas kernels: none -> 8.54 us  [the longest x1 6.96 us: partial_vertices(): pl.pallas_call(vertex_kernel, out_shape=(out, out), in_specs=[hbm] * 7, o...]
    dot_general x1 -> x0, matrix products: 7.15 us -> none  [shards(): jnp.einsum('pncom,epncw->oemw', table, g_wan, preferred_element_type=f32)]
    all_to_all x1, blocking collectives: 17.7 us -> 14.8 us  [shards(): found = lax.all_to_all(root.astype(SENT), ('z', 'y'), 0, 0, tiled=True)]
    reshape x6 -> x0, local copies, waits for them, and re-layouts: 2.39 us -> none  [the longest x3 1.52 us: shards(): vert.reshape(2, e, modes, W, W).transpose(3, 1, 0, 2, 4).reshape(W, -1, 128)]
  transfers between devices with their start and end apart: 4 -> 4, of which waited for: 4 -> 4; matrix products, arithmetic and copies ran while one was open for 0% -> 1% of each run, Pallas kernels for 4% -> 5%
where the time goes in v3:
time: 73.1 us; the launch traced here: 72.8 us
  waiting for transfers between devices  21.5 us (29%)
  Pallas kernels  19.5 us (27%)
  blocking collectives  14.8 us (20%)
  starting transfers between devices  14.2 us (19%)
  local copies, waits for them, and re-layouts  1.67 us (2%)
  other arithmetic  1 us (1%)
    all_to_all x1, blocking collectives, shards(): found = lax.all_to_all(root.astype(SENT), ('z', 'y'), 0, 0, tiled=True)  14.8 us
    all_to_all x1, waiting for transfers between devices, shards(): moved = lax.all_to_all(sent, ('z', 'y'), 0, 0, tiled=True)  11.6 us
    all_to_all x1, starting transfers between devices, shards(): moved = lax.all_to_all(sent, ('z', 'y'), 0, 0, tiled=True)  11.5 us
    pallas_call x1, Pallas kernels, strengths(): pl.pallas_call(lambda *refs: strength_kernel(modes, scale, *refs), out_sh...  7.41 us
    pallas_call x1, Pallas kernels, partial_vertices(): pl.pallas_call(vertex_kernel, out_shape=(out, out), in_specs=[hbm] * 7, o...  6.96 us
    ppermute x1, waiting for transfers between devices, shards(): passed = lax.ppermute((mine[0] + core_part[0]).astype(bf16), 'xl', SWAP)  6.12 us
    pallas_call x1, Pallas kernels, strengths(): pl.pallas_call(own_kernel, out_shape=pltpu.VMEM((cols, early), f32), in_s...  3.54 us
    ppermute x1, waiting for transfers between devices, shards(): core_part = lax.ppermute(theirs, 'core', SWAP)  2.27 us
  transfers between devices with their start and end apart: 4, of which 4 were waited for; matrix products, arithmetic and copies ran while one was open for 1% of the time, Pallas kernels for 5%

profile of v3, /device:TPU:6, one launch (start us, length us, event | category | flops | bytes accessed | tf_op | source)
XLA Modules:
  0.0 72.8 jit_solution(2194316158901645927)
XLA Ops:
  0.0 7.0 %vertices.1 = (f32[2,96,1024]{2,1,0:T(8,128)S(1)}, f32[2,96,1024]{2,1,0:T(8,128)S(1)}) custom-call(s32[3]{0:T(128)} %q_hbm.1, s32[3,12]{1,0:T(4,128)} %cells_hbm.1, f32[2,64]{1,0:T(2,128)} %constant.24.clone.trig_hbm, f32[2,48,48]{2,1,0:T(8,128)} %eig_hbm.1, f32[1,48]{1,0:T(1,128)} %bitcast.7, s32[96,8]{1,0:T(8,128)} %constant.25.clone.rows_hbm, ...), custom_call_target="tpu_custom_call" | custom-call | flops 905969664 | bytes 9437184 | tf_op jit(solution)/shard_map/vertices/pallas_call | solution.py:126
  7.0 0.1 collective-permute-start
  7.1 2.3 %collective-permute-done.core_ref = f32[2,96,1024]{2,1,0:T(8,128)S(1)} collective-permute-done((f32[2,96,1024]{2,1,0:T(8,128)S(1)}, f32[2,96,1024]{2,1,0:T(8,128)S(1)}, u32[]{:S(2)}, u32[]{:S(2)}) %collective-permute-start) | collective-permute-done | bytes 786464 | tf_op jit(solution)/shard_map/ppermute | solution.py:315
  9.4 0.9 %collective-permute-start.1 = (bf16[96,1024]{1,0:T(8,128)(2,1)S(1)}, bf16[96,1024]{1,0:T(8,128)(2,1)S(1)}, u32[]{:S(2)}, u32[]{:S(2)}) collective-permute-start(bf16[96,1024]{1,0:T(8,128)(2,1)S(1)} %fusion.1), channel_id=1, source_target_pairs={{0,128},{128,0},{1,129},{129,1},{2,130},{130,2},{3,131},{131,3},{4... | collective-permute-start | bytes 589832 | tf_op jit(solution)/shard_map/ppermute | solution.py:316
  10.3 6.1 %collective-permute-done.1.passed_ref = bf16[96,1024]{1,0:T(8,128)(2,1)S(1)} collective-permute-done((bf16[96,1024]{1,0:T(8,128)(2,1)S(1)}, bf16[96,1024]{1,0:T(8,128)(2,1)S(1)}, u32[]{:S(2)}, u32[]{:S(2)}) %collective-permute-start.1) | collective-permute-done | bytes 196640 | tf_op jit(solution)/shard_map/ppermute | solution.py:316
  16.4 0.0 copy-start
  16.4 0.7 copy-done
  17.1 0.8 %pack.1 = bf16[32,30,128]{2,1,0:T(8,128)(2,1)} custom-call(f32[2,96,1024]{2,1,0:T(8,128)S(1)} %get-tuple-element.7.mine_ref, f32[2,96,1024]{2,1,0:T(8,128)S(1)} %collective-permute-done.core_ref, bf16[96,1024]{1,0:T(8,128)(2,1)S(1)} %collective-permute-done.1.passed_ref, s32[3,256]{1,0:T(4,128)S(1)} %copy-done), custom_call_target="tpu_custom_call" | custom-call | tf_op jit(solution)/shard_map/pack/pallas_call | solution.py:271
  17.9 11.5 %all-to-all-start = ((bf16[32,30,128]{2,1,0:T(8,128)(2,1)}), bf16[32,30,128]{2,1,0:T(8,128)(2,1)S(1)}, u32[]{:S(2)}, u32[]{:S(2)}) async-start(bf16[32,30,128]{2,1,0:T(8,128)(2,1)} %pack.1), calls=%async_computation | async-start | bytes 524288 | tf_op jit(solution)/shard_map/all_to_all | solution.py:319
  29.4 0.7 convert_element_type.21
  30.1 11.6 %all-to-all-done = bf16[32,30,128]{2,1,0:T(8,128)(2,1)S(1)} async-done(((bf16[32,30,128]{2,1,0:T(8,128)(2,1)}), bf16[32,30,128]{2,1,0:T(8,128)(2,1)S(1)}, u32[]{:S(2)}, u32[]{:S(2)}) %all-to-all-start) | async-done | bytes 245792 | tf_op jit(solution)/shard_map/all_to_all | solution.py:319
  41.7 0.2 reshape.15.vert_ref.refs_0_
  41.9 0.1 reshape.16
  42.0 1.7 %collective-permute-start.2 = (bf16[128,768]{1,0:T(8,128)(2,1)S(1)}, bf16[128,768]{1,0:T(8,128)(2,1)S(1)}, u32[]{:S(2)}, u32[]{:S(2)}) collective-permute-start(bf16[128,768]{1,0:T(8,128)(2,1)S(1)} %reshape.15.vert_ref.refs_0_), channel_id=1, source_target_pairs={{0,32},{32,0},{1,33},{33,1},{2,34},{34,2},{3,35},{35,3},{4,36},{36... | collective-permute-start | bytes 589832 | tf_op jit(solution)/shard_map/ppermute | solution.py:322
  43.7 0.0 copy-start.1
  43.7 0.7 copy-done.1
  44.4 3.5 %own.1.refs_5_ = f32[768,6144]{1,0:T(8,128)S(1)} custom-call(bf16[128,768]{1,0:T(8,128)(2,1)S(1)} %reshape.15.vert_ref.refs_0_, bf16[8,8192]{1,0:T(8,128)(2,1)S(1)} %pad.8.kp_ref.refs_2_, bf16[8,256]{1,0:T(8,128)(2,1)S(1)} %fusion.4.el_ref.refs_3_, f32[8,128]{1,0:T(8,128)S(1)} %copy-done.1), custom_call_target="tpu_custom_call" | custom-call | flops 2415919104 | bytes 18874368 | tf_op jit(solution)/shard_map/own/pallas_call | solution.py:222
  47.9 1.5 %collective-permute-done.2.refs_1_ = bf16[128,768]{1,0:T(8,128)(2,1)S(1)} collective-permute-done((bf16[128,768]{1,0:T(8,128)(2,1)S(1)}, bf16[128,768]{1,0:T(8,128)(2,1)S(1)}, u32[]{:S(2)}, u32[]{:S(2)}) %collective-permute-start.2) | collective-permute-done | bytes 196640 | tf_op jit(solution)/shard_map/ppermute | solution.py:322
  49.4 7.4 %strengths.1 = f32[32,24,128]{2,1,0:T(8,128)S(1)} custom-call(bf16[128,768]{1,0:T(8,128)(2,1)S(1)} %reshape.15.vert_ref.refs_0_, bf16[128,768]{1,0:T(8,128)(2,1)S(1)} %collective-permute-done.2.refs_1_, bf16[8,8192]{1,0:T(8,128)(2,1)S(1)} %pad.8.kp_ref.refs_2_, bf16[8,256]{1,0:T(8,128)(2,1)S(1)} %fusion.4.el_ref.refs_3_, f32[8,128]{1,0:T(8,128)S(1)} %copy-done.1, ...), custom_call_target="tpu_custom_call" | custom-call | flops 6442450944 | bytes 18874368 | tf_op jit(solution)/shard_map/strengths/pallas_call | solution.py:237
  56.9 0.2 multiply_convert_fusion
  57.1 14.8 %all_to_all.10 = f16[32,24,128]{2,1,0:T(8,128)(2,1)S(1)} all-to-all(f16[32,24,128]{2,1,0:T(8,128)(2,1)S(1)} %multiply_convert_fusion), channel_id=1, replica_groups=mesh['xl'=2,'core'=2,'xh'=2,'z'=8,'y'=4] {'z','y'}, dimensions={0} | all-to-all | bytes 393216 | tf_op jit(solution)/shard_map/all_to_all | solution.py:338
  72.0 0.8 %unpack.1 = f32[12,32,256]{2,1,0:T(8,128)} custom-call(f32[32,24,128]{2,1,0:T(8,128)S(1)} %convert_element_type.23.in_ref), custom_call_target="tpu_custom_call" | custom-call | tf_op jit(solution)/shard_map/unpack/pallas_call | solution.py:297
  (7 shorter events, 0.1 us)
Async XLA Ops:
  7.0 2.4 %collective-permute-start = (f32[2,96,1024]{2,1,0:T(8,128)S(1)}, f32[2,96,1024]{2,1,0:T(8,128)S(1)}, u32[]{:S(2)}, u32[]{:S(2)}) collective-permute-start(f32[2,96,1024]{2,1,0:T(8,128)S(1)} %get-tuple-element.8), channel_id=1, source_target_pairs={{0,64},{64,0},{1,65},{65,1},{2,66},{66,2},{3,67},{67,3},{4,68},{68... | collective-permute-start | bytes 2359304 | tf_op jit(solution)/shard_map/ppermute | solution.py:315
  9.4 7.0 %collective-permute-start.1 = (bf16[96,1024]{1,0:T(8,128)(2,1)S(1)}, bf16[96,1024]{1,0:T(8,128)(2,1)S(1)}, u32[]{:S(2)}, u32[]{:S(2)}) collective-permute-start(bf16[96,1024]{1,0:T(8,128)(2,1)S(1)} %fusion.1), channel_id=1, source_target_pairs={{0,128},{128,0},{1,129},{129,1},{2,130},{130,2},{3,131},{131,3},{4... | collective-permute-start | bytes 589832 | tf_op jit(solution)/shard_map/ppermute | solution.py:316
  16.4 0.7 copy-start
  17.9 23.8 %all-to-all-start = ((bf16[32,30,128]{2,1,0:T(8,128)(2,1)}), bf16[32,30,128]{2,1,0:T(8,128)(2,1)S(1)}, u32[]{:S(2)}, u32[]{:S(2)}) async-start(bf16[32,30,128]{2,1,0:T(8,128)(2,1)} %pack.1), calls=%async_computation | async-start | bytes 524288 | tf_op jit(solution)/shard_map/all_to_all | solution.py:319
  42.0 7.4 %collective-permute-start.2 = (bf16[128,768]{1,0:T(8,128)(2,1)S(1)}, bf16[128,768]{1,0:T(8,128)(2,1)S(1)}, u32[]{:S(2)}, u32[]{:S(2)}) collective-permute-start(bf16[128,768]{1,0:T(8,128)(2,1)S(1)} %reshape.15.vert_ref.refs_0_), channel_id=1, source_target_pairs={{0,32},{32,0},{1,33},{33,1},{2,34},{34,2},{3,35},{35,3},{4,36},{36... | collective-permute-start | bytes 589832 | tf_op jit(solution)/shard_map/ppermute | solution.py:322
  43.7 0.7 copy-start.1

commit v4 on v3

--- a/solution.py
+++ b/solution.py
@@ -15,9 +15,9 @@
 SWAP = [(0, 1), (1, 0)]
 CELLS = 128
 K_STEP = 1024
-K_BLOCK = 2048
-EARLY = 6144
-VMEM_MIB = 32
+K_BLOCK = 1024
+EARLY = 8192
+VMEM_MIB = 26
 TRIO = 3
 SENT = jnp.float16
 ROOT_SCALE = 64.0
@@ -93,17 +93,18 @@
         copy.start()
     for copy in first:
         copy.wait()
+    copies[0].wait()
     fill_coupling(q_ref, cells_ref, trig_ref, eig_ref, omega_ref, rows_ref, table)
     part = 2 * TRIO
 
     def flatten(e):
-        copies[e].wait()
         for p in range(p_count):
             flat[e % 2, p * 2 * nu : (p + 1) * 2 * nu, :] = held[e, p].reshape(2 * nu, W * W)
 
     flatten(0)
     for e in range(e_count):
         if e + 1 < e_count:
+            copies[e + 1].wait()
             flatten(e + 1)
         found = jnp.dot(table[...], flat[e % 2], preferred_element_type=jnp.float32)
         row = 0
@@ -255,7 +256,6 @@
     lanes = kp_ref.shape[1]
     halves = [slice(lane, lane + 128) for lane in range(0, lanes, 128)]
     kp = jnp.concatenate([kp_ref[d : d + 1, at] for d in range(3) for at in halves])
-    kp = kp.astype(jnp.float32).astype(jnp.bfloat16)
     rows = out_ref.shape[1] - kp.shape[0]
     total = mine_ref[1] + core_ref[1] + passed_ref[...].astype(jnp.float32)
     total = total.astype(jnp.bfloat16)
@@ -270,7 +270,7 @@
     vmem = pl.BlockSpec(memory_space=pltpu.VMEM)
     return pl.pallas_call(
         pack_kernel,
-        out_shape=jax.ShapeDtypeStruct((W, rows, 128), jnp.bfloat16),
+        out_shape=pltpu.VMEM((W, rows, 128), jnp.bfloat16),
         in_specs=[vmem] * 4,
         out_specs=vmem,
         compiler_params=pltpu.CompilerParams(vmem_limit_bytes=16 * 2**20),
@@ -314,7 +314,7 @@
     theirs, mine = partial_vertices(q_point, ph_cells, eigvec, omega, g_wan)
     core_part = lax.ppermute(theirs, "core", SWAP)
     passed = lax.ppermute((mine[0] + core_part[0]).astype(bf16), "xl", SWAP)
-    sent = pack(mine, core_part, passed, kpoints)
+    sent = pack(mine, core_part, passed, kpoints.astype(bf16))
     rows = passed.shape[0] // 4
     moved = lax.all_to_all(sent, ("z", "y"), 0, 0, tiled=True)
     own = moved[:, :rows].reshape(W * e, 2 * modes * W)
@@ -331,7 +331,8 @@
     )
     el = jnp.pad(el, ((0, 5), (0, 0)))
     kp = jnp.pad(kp, ((0, 5), (0, 0)))
-    trig = np.pad(trig_table(128), ((0, 6), (0, 0)))
+    angle = (jnp.arange(128) % KGRID).astype(f32) * (2.0 * math.pi / KGRID)
+    trig = jnp.pad(jnp.stack([jnp.cos(angle), jnp.sin(angle)]), ((0, 6), (0, 0)))
     scale = 1.0 / float(el_cells.shape[1] * nu * W)
     found = strengths(own, other, kp, el, trig, modes, scale, W)
     root = jnp.sqrt(jnp.sqrt(found)) * ROOT_SCALE

time: 73.1 us -> 71.7 us (0.981)
  local copies, waits for them, and re-layouts: 1.67 us -> 0.31 us
  waiting for transfers between devices: 21.5 us -> 20.4 us
  other arithmetic: 1 us -> 1.74 us
    unnamed x4 -> x0, local copies, waits for them, and re-layouts: 1.37 us -> none
    pallas_call x1, Pallas kernels: 3.54 us -> 4.55 us  [strengths(): pl.pallas_call(own_kernel, out_shape=pltpu.VMEM((cols, early), f32), in_s...]
  transfers between devices with their start and end apart: 4 -> 4, of which waited for: 4 -> 4; matrix products, arithmetic and copies ran while one was open for 1% -> 2% of each run, Pallas kernels for 5% -> 6%
where the time goes in v4:
time: 71.7 us; the launch traced here: 71.4 us
  waiting for transfers between devices  20.4 us (28%)
  Pallas kernels  19.8 us (28%)
  blocking collectives  14.9 us (21%)
  starting transfers between devices  14.2 us (20%)
  other arithmetic  1.74 us (2%)
    all_to_all x1, blocking collectives, shards(): found = lax.all_to_all(root.astype(SENT), ('z', 'y'), 0, 0, tiled=True)  14.9 us
    all_to_all x1, waiting for transfers between devices, shards(): moved = lax.all_to_all(sent, ('z', 'y'), 0, 0, tiled=True)  11.5 us
    all_to_all x1, starting transfers between devices, shards(): moved = lax.all_to_all(sent, ('z', 'y'), 0, 0, tiled=True)  11.5 us
    pallas_call x1, Pallas kernels, partial_vertices(): pl.pallas_call(vertex_kernel, out_shape=(out, out), in_specs=[hbm] * 7, o...  6.85 us
    pallas_call x1, Pallas kernels, strengths(): pl.pallas_call(lambda *refs: strength_kernel(modes, scale, *refs), out_sh...  6.78 us
    ppermute x1, waiting for transfers between devices, shards(): passed = lax.ppermute((mine[0] + core_part[0]).astype(bf16), 'xl', SWAP)  5.42 us
    pallas_call x1, Pallas kernels, strengths(): pl.pallas_call(own_kernel, out_shape=pltpu.VMEM((cols, early), f32), in_s...  4.55 us
    ppermute x1, waiting for transfers between devices, shards(): core_part = lax.ppermute(theirs, 'core', SWAP)  2.27 us
  transfers between devices with their start and end apart: 4, of which 4 were waited for; matrix products, arithmetic and copies ran while one was open for 2% of the time, Pallas kernels for 6%

profile of v4, /device:TPU:6, one launch (start us, length us, event | category | flops | bytes accessed | tf_op | source)
XLA Modules:
  0.0 71.4 jit_solution(16967525581317542109)
XLA Ops:
  0.0 6.9 %vertices.1 = (f32[2,96,1024]{2,1,0:T(8,128)S(1)}, f32[2,96,1024]{2,1,0:T(8,128)S(1)}) custom-call(s32[3]{0:T(128)} %q_hbm.1, s32[3,12]{1,0:T(4,128)} %cells_hbm.1, f32[2,64]{1,0:T(2,128)} %constant.41.clone.trig_hbm, f32[2,48,48]{2,1,0:T(8,128)} %eig_hbm.1, f32[1,48]{1,0:T(1,128)} %bitcast.7, s32[96,8]{1,0:T(8,128)} %constant.42.clone.rows_hbm, ...), custom_call_target="tpu_custom_call" | custom-call | flops 905969664 | bytes 9437184 | tf_op jit(solution)/shard_map/vertices/pallas_call | solution.py:127
  6.9 0.1 collective-permute-start
  7.0 2.3 %collective-permute-done.core_ref = f32[2,96,1024]{2,1,0:T(8,128)S(1)} collective-permute-done((f32[2,96,1024]{2,1,0:T(8,128)S(1)}, f32[2,96,1024]{2,1,0:T(8,128)S(1)}, u32[]{:S(2)}, u32[]{:S(2)}) %collective-permute-start) | collective-permute-done | bytes 786464 | tf_op jit(solution)/shard_map/ppermute | solution.py:315
  9.3 0.9 %collective-permute-start.1 = (bf16[96,1024]{1,0:T(8,128)(2,1)S(1)}, bf16[96,1024]{1,0:T(8,128)(2,1)S(1)}, u32[]{:S(2)}, u32[]{:S(2)}) collective-permute-start(bf16[96,1024]{1,0:T(8,128)(2,1)S(1)} %fusion.1), channel_id=1, source_target_pairs={{0,128},{128,0},{1,129},{129,1},{2,130},{130,2},{3,131},{131,3},{4... | collective-permute-start | bytes 589832 | tf_op jit(solution)/shard_map/ppermute | solution.py:316
  10.2 0.7 convert_element_type.42.kp_ref
  10.9 5.4 %collective-permute-done.1.passed_ref = bf16[96,1024]{1,0:T(8,128)(2,1)S(1)} collective-permute-done((bf16[96,1024]{1,0:T(8,128)(2,1)S(1)}, bf16[96,1024]{1,0:T(8,128)(2,1)S(1)}, u32[]{:S(2)}, u32[]{:S(2)}) %collective-permute-start.1) | collective-permute-done | bytes 196640 | tf_op jit(solution)/shard_map/ppermute | solution.py:316
  16.3 0.8 %pack.1 = bf16[32,30,128]{2,1,0:T(8,128)(2,1)} custom-call(f32[2,96,1024]{2,1,0:T(8,128)S(1)} %get-tuple-element.7.mine_ref, f32[2,96,1024]{2,1,0:T(8,128)S(1)} %collective-permute-done.core_ref, bf16[96,1024]{1,0:T(8,128)(2,1)S(1)} %collective-permute-done.1.passed_ref, bf16[3,256]{1,0:T(4,128)(2,1)S(1)} %convert_element_type.42.kp_ref), custom_call_target="tpu_custom_call" | custom-call | tf_op jit(solution)/shard_map/pack/pallas_call | solution.py:271
  17.1 11.5 %all-to-all-start = ((bf16[32,30,128]{2,1,0:T(8,128)(2,1)}), bf16[32,30,128]{2,1,0:T(8,128)(2,1)S(1)}, u32[]{:S(2)}, u32[]{:S(2)}) async-start(bf16[32,30,128]{2,1,0:T(8,128)(2,1)} %pack.1), calls=%async_computation | async-start | bytes 524288 | tf_op jit(solution)/shard_map/all_to_all | solution.py:319
  28.6 0.7 convert_element_type.43
  29.4 11.5 %all-to-all-done = bf16[32,30,128]{2,1,0:T(8,128)(2,1)S(1)} async-done(((bf16[32,30,128]{2,1,0:T(8,128)(2,1)}), bf16[32,30,128]{2,1,0:T(8,128)(2,1)S(1)}, u32[]{:S(2)}, u32[]{:S(2)}) %all-to-all-start) | async-done | bytes 245792 | tf_op jit(solution)/shard_map/all_to_all | solution.py:319
  40.9 0.2 reshape.50.vert_ref.refs_0_
  41.2 0.1 reshape.51
  41.2 1.7 %collective-permute-start.2 = (bf16[128,768]{1,0:T(8,128)(2,1)S(1)}, bf16[128,768]{1,0:T(8,128)(2,1)S(1)}, u32[]{:S(2)}, u32[]{:S(2)}) collective-permute-start(bf16[128,768]{1,0:T(8,128)(2,1)S(1)} %reshape.50.vert_ref.refs_0_), channel_id=1, source_target_pairs={{0,32},{32,0},{1,33},{33,1},{2,34},{34,2},{3,35},{35,3},{4,36},{36... | collective-permute-start | bytes 589832 | tf_op jit(solution)/shard_map/ppermute | solution.py:322
  42.9 4.6 %own.1.refs_5_ = f32[768,8192]{1,0:T(8,128)S(1)} custom-call(bf16[128,768]{1,0:T(8,128)(2,1)S(1)} %reshape.50.vert_ref.refs_0_, bf16[8,8192]{1,0:T(8,128)(2,1)S(1)} %pad.12.kp_ref.refs_2_, bf16[8,256]{1,0:T(8,128)(2,1)S(1)} %fusion.4.el_ref.refs_3_, f32[8,128]{1,0:T(8,128)S(1)} %select_maximum_fusion.trig_ref.refs_4_), custom_call_target="tpu_custom_call" | custom-call | flops 3221225472 | bytes 25165824 | tf_op jit(solution)/shard_map/own/pallas_call | solution.py:223
  47.5 1.2 %collective-permute-done.2.refs_1_ = bf16[128,768]{1,0:T(8,128)(2,1)S(1)} collective-permute-done((bf16[128,768]{1,0:T(8,128)(2,1)S(1)}, bf16[128,768]{1,0:T(8,128)(2,1)S(1)}, u32[]{:S(2)}, u32[]{:S(2)}) %collective-permute-start.2) | collective-permute-done | bytes 196640 | tf_op jit(solution)/shard_map/ppermute | solution.py:322
  48.7 6.8 %strengths.1 = f32[32,24,128]{2,1,0:T(8,128)S(1)} custom-call(bf16[128,768]{1,0:T(8,128)(2,1)S(1)} %reshape.50.vert_ref.refs_0_, bf16[128,768]{1,0:T(8,128)(2,1)S(1)} %collective-permute-done.2.refs_1_, bf16[8,8192]{1,0:T(8,128)(2,1)S(1)} %pad.12.kp_ref.refs_2_, bf16[8,256]{1,0:T(8,128)(2,1)S(1)} %fusion.4.el_ref.refs_3_, ...), custom_call_target="tpu_custom_call" | custom-call | flops 6442450944 | bytes 25165824 | tf_op jit(solution)/shard_map/strengths/pallas_call | solution.py:238
  55.4 0.2 multiply_convert_fusion
  55.7 14.9 %all_to_all.10 = f16[32,24,128]{2,1,0:T(8,128)(2,1)S(1)} all-to-all(f16[32,24,128]{2,1,0:T(8,128)(2,1)S(1)} %multiply_convert_fusion), channel_id=1, replica_groups=mesh['xl'=2,'core'=2,'xh'=2,'z'=8,'y'=4] {'z','y'}, dimensions={0} | all-to-all | bytes 393216 | tf_op jit(solution)/shard_map/all_to_all | solution.py:339
  70.6 0.8 %unpack.1 = f32[12,32,256]{2,1,0:T(8,128)} custom-call(f32[32,24,128]{2,1,0:T(8,128)S(1)} %convert_element_type.46.in_ref), custom_call_target="tpu_custom_call" | custom-call | tf_op jit(solution)/shard_map/unpack/pallas_call | solution.py:297
  (9 shorter events, 0.2 us)
Async XLA Ops:
  6.9 2.4 %collective-permute-start = (f32[2,96,1024]{2,1,0:T(8,128)S(1)}, f32[2,96,1024]{2,1,0:T(8,128)S(1)}, u32[]{:S(2)}, u32[]{:S(2)}) collective-permute-start(f32[2,96,1024]{2,1,0:T(8,128)S(1)} %get-tuple-element.8), channel_id=1, source_target_pairs={{0,64},{64,0},{1,65},{65,1},{2,66},{66,2},{3,67},{67,3},{4,68},{68... | collective-permute-start | bytes 2359304 | tf_op jit(solution)/shard_map/ppermute | solution.py:315
  9.3 7.0 %collective-permute-start.1 = (bf16[96,1024]{1,0:T(8,128)(2,1)S(1)}, bf16[96,1024]{1,0:T(8,128)(2,1)S(1)}, u32[]{:S(2)}, u32[]{:S(2)}) collective-permute-start(bf16[96,1024]{1,0:T(8,128)(2,1)S(1)} %fusion.1), channel_id=1, source_target_pairs={{0,128},{128,0},{1,129},{129,1},{2,130},{130,2},{3,131},{131,3},{4... | collective-permute-start | bytes 589832 | tf_op jit(solution)/shard_map/ppermute | solution.py:316
  17.1 23.8 %all-to-all-start = ((bf16[32,30,128]{2,1,0:T(8,128)(2,1)}), bf16[32,30,128]{2,1,0:T(8,128)(2,1)S(1)}, u32[]{:S(2)}, u32[]{:S(2)}) async-start(bf16[32,30,128]{2,1,0:T(8,128)(2,1)} %pack.1), calls=%async_computation | async-start | bytes 524288 | tf_op jit(solution)/shard_map/all_to_all | solution.py:319
  41.2 7.4 %collective-permute-start.2 = (bf16[128,768]{1,0:T(8,128)(2,1)S(1)}, bf16[128,768]{1,0:T(8,128)(2,1)S(1)}, u32[]{:S(2)}, u32[]{:S(2)}) collective-permute-start(bf16[128,768]{1,0:T(8,128)(2,1)S(1)} %reshape.50.vert_ref.refs_0_), channel_id=1, source_target_pairs={{0,32},{32,0},{1,33},{33,1},{2,34},{34,2},{3,35},{35,3},{4,36},{36... | collective-permute-start | bytes 589832 | tf_op jit(solution)/shard_map/ppermute | solution.py:322

commit v5 on v4

--- a/solution.py
+++ b/solution.py
@@ -15,10 +15,11 @@
 SWAP = [(0, 1), (1, 0)]
 CELLS = 128
 K_STEP = 1024
-K_BLOCK = 1024
+K_BLOCK = 2048
 EARLY = 8192
 VMEM_MIB = 26
 TRIO = 3
+PIECES = 3
 SENT = jnp.float16
 ROOT_SCALE = 64.0
 
@@ -88,12 +89,24 @@
         pltpu.make_async_copy(source, target, small.at[i])
         for i, (source, target) in enumerate(zip(sources, targets))
     ]
-    copies = [pltpu.make_async_copy(g_ref.at[e], held.at[e], sems.at[e]) for e in range(e_count)]
-    for copy in first + copies:
+    cut = p_count // PIECES
+    copies = [
+        [
+            pltpu.make_async_copy(
+                g_ref.at[e, pl.ds(piece * cut, cut)],
+                held.at[e, pl.ds(piece * cut, cut)],
+                sems.at[e, piece],
+            )
+            for piece in range(PIECES)
+        ]
+        for e in range(e_count)
+    ]
+    for copy in first + sum(copies, []):
         copy.start()
     for copy in first:
         copy.wait()
-    copies[0].wait()
+    for copy in copies[0]:
+        copy.wait()
     fill_coupling(q_ref, cells_ref, trig_ref, eig_ref, omega_ref, rows_ref, table)
     part = 2 * TRIO
 
@@ -104,7 +117,8 @@
     flatten(0)
     for e in range(e_count):
         if e + 1 < e_count:
-            copies[e + 1].wait()
+            for copy in copies[e + 1]:
+                copy.wait()
             flatten(e + 1)
         found = jnp.dot(table[...], flat[e % 2], preferred_element_type=jnp.float32)
         row = 0
@@ -140,7 +154,7 @@
             pltpu.VMEM((2, p * 2 * nu, W * W), jnp.bfloat16),
             pltpu.VMEM((rows.shape[0], p * 2 * nu), jnp.bfloat16),
             pltpu.SemaphoreType.DMA((6,)),
-            pltpu.SemaphoreType.DMA((e,)),
+            pltpu.SemaphoreType.DMA((e, PIECES)),
         ],
         compiler_params=pltpu.CompilerParams(vmem_limit_bytes=40 * 2**20),
         cost_estimate=pl.CostEstimate(

time: 71.7 us -> 72.2 us (level)
  no operation moved by 1% of the time
where the time goes in v5:
time: 72.2 us; the launch traced here: 71.9 us
  waiting for transfers between devices  20.4 us (28%)
  Pallas kernels  20.3 us (28%)
  blocking collectives  14.8 us (20%)
  starting transfers between devices  14.2 us (20%)
  other arithmetic  1.74 us (2%)
    all_to_all x1, blocking collectives, shards(): found = lax.all_to_all(root.astype(SENT), ('z', 'y'), 0, 0, tiled=True)  14.8 us
    all_to_all x1, waiting for transfers between devices, shards(): moved = lax.all_to_all(sent, ('z', 'y'), 0, 0, tiled=True)  11.5 us
    all_to_all x1, starting transfers between devices, shards(): moved = lax.all_to_all(sent, ('z', 'y'), 0, 0, tiled=True)  11.5 us
    pallas_call x1, Pallas kernels, partial_vertices(): pl.pallas_call(vertex_kernel, out_shape=(out, out), in_specs=[hbm] * 7, o...  7.39 us
    pallas_call x1, Pallas kernels, strengths(): pl.pallas_call(lambda *refs: strength_kernel(modes, scale, *refs), out_sh...  6.77 us
    ppermute x1, waiting for transfers between devices, shards(): passed = lax.ppermute((mine[0] + core_part[0]).astype(bf16), 'xl', SWAP)  5.42 us
    pallas_call x1, Pallas kernels, strengths(): pl.pallas_call(own_kernel, out_shape=pltpu.VMEM((cols, early), f32), in_s...  4.55 us
    ppermute x1, waiting for transfers between devices, shards(): core_part = lax.ppermute(theirs, 'core', SWAP)  2.27 us
  transfers between devices with their start and end apart: 4, of which 4 were waited for; matrix products, arithmetic and copies ran while one was open for 2% of the time, Pallas kernels for 6%

profile of v5, /device:TPU:6, one launch (start us, length us, event | category | flops | bytes accessed | tf_op | source)
XLA Modules:
  0.0 71.9 jit_solution(5462254415382601619)
XLA Ops:
  0.0 7.4 %vertices.1 = (f32[2,96,1024]{2,1,0:T(8,128)S(1)}, f32[2,96,1024]{2,1,0:T(8,128)S(1)}) custom-call(s32[3]{0:T(128)} %q_hbm.1, s32[3,12]{1,0:T(4,128)} %cells_hbm.1, f32[2,64]{1,0:T(2,128)} %constant.41.clone.trig_hbm, f32[2,48,48]{2,1,0:T(8,128)} %eig_hbm.1, f32[1,48]{1,0:T(1,128)} %bitcast.7, s32[96,8]{1,0:T(8,128)} %constant.42.clone.rows_hbm, ...), custom_call_target="tpu_custom_call" | custom-call | flops 905969664 | bytes 9437184 | tf_op jit(solution)/shard_map/vertices/pallas_call | solution.py:141
  7.4 0.1 collective-permute-start
  7.5 2.3 %collective-permute-done.core_ref = f32[2,96,1024]{2,1,0:T(8,128)S(1)} collective-permute-done((f32[2,96,1024]{2,1,0:T(8,128)S(1)}, f32[2,96,1024]{2,1,0:T(8,128)S(1)}, u32[]{:S(2)}, u32[]{:S(2)}) %collective-permute-start) | collective-permute-done | bytes 786464 | tf_op jit(solution)/shard_map/ppermute | solution.py:329
  9.8 0.9 %collective-permute-start.1 = (bf16[96,1024]{1,0:T(8,128)(2,1)S(1)}, bf16[96,1024]{1,0:T(8,128)(2,1)S(1)}, u32[]{:S(2)}, u32[]{:S(2)}) collective-permute-start(bf16[96,1024]{1,0:T(8,128)(2,1)S(1)} %fusion.1), channel_id=1, source_target_pairs={{0,128},{128,0},{1,129},{129,1},{2,130},{130,2},{3,131},{131,3},{4... | collective-permute-start | bytes 589832 | tf_op jit(solution)/shard_map/ppermute | solution.py:330
  10.7 0.7 convert_element_type.42.kp_ref
  11.4 5.4 %collective-permute-done.1.passed_ref = bf16[96,1024]{1,0:T(8,128)(2,1)S(1)} collective-permute-done((bf16[96,1024]{1,0:T(8,128)(2,1)S(1)}, bf16[96,1024]{1,0:T(8,128)(2,1)S(1)}, u32[]{:S(2)}, u32[]{:S(2)}) %collective-permute-start.1) | collective-permute-done | bytes 196640 | tf_op jit(solution)/shard_map/ppermute | solution.py:330
  16.8 0.8 %pack.1 = bf16[32,30,128]{2,1,0:T(8,128)(2,1)} custom-call(f32[2,96,1024]{2,1,0:T(8,128)S(1)} %get-tuple-element.7.mine_ref, f32[2,96,1024]{2,1,0:T(8,128)S(1)} %collective-permute-done.core_ref, bf16[96,1024]{1,0:T(8,128)(2,1)S(1)} %collective-permute-done.1.passed_ref, bf16[3,256]{1,0:T(4,128)(2,1)S(1)} %convert_element_type.42.kp_ref), custom_call_target="tpu_custom_call" | custom-call | tf_op jit(solution)/shard_map/pack/pallas_call | solution.py:285
  17.6 11.5 %all-to-all-start = ((bf16[32,30,128]{2,1,0:T(8,128)(2,1)}), bf16[32,30,128]{2,1,0:T(8,128)(2,1)S(1)}, u32[]{:S(2)}, u32[]{:S(2)}) async-start(bf16[32,30,128]{2,1,0:T(8,128)(2,1)} %pack.1), calls=%async_computation | async-start | bytes 524288 | tf_op jit(solution)/shard_map/all_to_all | solution.py:333
  29.1 0.7 convert_element_type.43
  29.9 11.5 %all-to-all-done = bf16[32,30,128]{2,1,0:T(8,128)(2,1)S(1)} async-done(((bf16[32,30,128]{2,1,0:T(8,128)(2,1)}), bf16[32,30,128]{2,1,0:T(8,128)(2,1)S(1)}, u32[]{:S(2)}, u32[]{:S(2)}) %all-to-all-start) | async-done | bytes 245792 | tf_op jit(solution)/shard_map/all_to_all | solution.py:333
  41.5 0.2 reshape.50.vert_ref.refs_0_
  41.7 0.1 reshape.51
  41.8 1.7 %collective-permute-start.2 = (bf16[128,768]{1,0:T(8,128)(2,1)S(1)}, bf16[128,768]{1,0:T(8,128)(2,1)S(1)}, u32[]{:S(2)}, u32[]{:S(2)}) collective-permute-start(bf16[128,768]{1,0:T(8,128)(2,1)S(1)} %reshape.50.vert_ref.refs_0_), channel_id=1, source_target_pairs={{0,32},{32,0},{1,33},{33,1},{2,34},{34,2},{3,35},{35,3},{4,36},{36... | collective-permute-start | bytes 589832 | tf_op jit(solution)/shard_map/ppermute | solution.py:336
  43.5 4.6 %own.1.refs_5_ = f32[768,8192]{1,0:T(8,128)S(1)} custom-call(bf16[128,768]{1,0:T(8,128)(2,1)S(1)} %reshape.50.vert_ref.refs_0_, bf16[8,8192]{1,0:T(8,128)(2,1)S(1)} %pad.12.kp_ref.refs_2_, bf16[8,256]{1,0:T(8,128)(2,1)S(1)} %fusion.4.el_ref.refs_3_, f32[8,128]{1,0:T(8,128)S(1)} %select_maximum_fusion.trig_ref.refs_4_), custom_call_target="tpu_custom_call" | custom-call | flops 3221225472 | bytes 25165824 | tf_op jit(solution)/shard_map/own/pallas_call | solution.py:237
  48.0 1.2 %collective-permute-done.2.refs_1_ = bf16[128,768]{1,0:T(8,128)(2,1)S(1)} collective-permute-done((bf16[128,768]{1,0:T(8,128)(2,1)S(1)}, bf16[128,768]{1,0:T(8,128)(2,1)S(1)}, u32[]{:S(2)}, u32[]{:S(2)}) %collective-permute-start.2) | collective-permute-done | bytes 196640 | tf_op jit(solution)/shard_map/ppermute | solution.py:336
  49.2 6.8 %strengths.1 = f32[32,24,128]{2,1,0:T(8,128)S(1)} custom-call(bf16[128,768]{1,0:T(8,128)(2,1)S(1)} %reshape.50.vert_ref.refs_0_, bf16[128,768]{1,0:T(8,128)(2,1)S(1)} %collective-permute-done.2.refs_1_, bf16[8,8192]{1,0:T(8,128)(2,1)S(1)} %pad.12.kp_ref.refs_2_, bf16[8,256]{1,0:T(8,128)(2,1)S(1)} %fusion.4.el_ref.refs_3_, ...), custom_call_target="tpu_custom_call" | custom-call | flops 6442450944 | bytes 25165824 | tf_op jit(solution)/shard_map/strengths/pallas_call | solution.py:252
  56.0 0.2 multiply_convert_fusion
  56.2 14.8 %all_to_all.10 = f16[32,24,128]{2,1,0:T(8,128)(2,1)S(1)} all-to-all(f16[32,24,128]{2,1,0:T(8,128)(2,1)S(1)} %multiply_convert_fusion), channel_id=1, replica_groups=mesh['xl'=2,'core'=2,'xh'=2,'z'=8,'y'=4] {'z','y'}, dimensions={0} | all-to-all | bytes 393216 | tf_op jit(solution)/shard_map/all_to_all | solution.py:353
  71.1 0.8 %unpack.1 = f32[12,32,256]{2,1,0:T(8,128)} custom-call(f32[32,24,128]{2,1,0:T(8,128)S(1)} %convert_element_type.46.in_ref), custom_call_target="tpu_custom_call" | custom-call | tf_op jit(solution)/shard_map/unpack/pallas_call | solution.py:311
  (9 shorter events, 0.2 us)
Async XLA Ops:
  7.4 2.4 %collective-permute-start = (f32[2,96,1024]{2,1,0:T(8,128)S(1)}, f32[2,96,1024]{2,1,0:T(8,128)S(1)}, u32[]{:S(2)}, u32[]{:S(2)}) collective-permute-start(f32[2,96,1024]{2,1,0:T(8,128)S(1)} %get-tuple-element.8), channel_id=1, source_target_pairs={{0,64},{64,0},{1,65},{65,1},{2,66},{66,2},{3,67},{67,3},{4,68},{68... | collective-permute-start | bytes 2359304 | tf_op jit(solution)/shard_map/ppermute | solution.py:329
  9.8 7.0 %collective-permute-start.1 = (bf16[96,1024]{1,0:T(8,128)(2,1)S(1)}, bf16[96,1024]{1,0:T(8,128)(2,1)S(1)}, u32[]{:S(2)}, u32[]{:S(2)}) collective-permute-start(bf16[96,1024]{1,0:T(8,128)(2,1)S(1)} %fusion.1), channel_id=1, source_target_pairs={{0,128},{128,0},{1,129},{129,1},{2,130},{130,2},{3,131},{131,3},{4... | collective-permute-start | bytes 589832 | tf_op jit(solution)/shard_map/ppermute | solution.py:330
  17.6 23.8 %all-to-all-start = ((bf16[32,30,128]{2,1,0:T(8,128)(2,1)}), bf16[32,30,128]{2,1,0:T(8,128)(2,1)S(1)}, u32[]{:S(2)}, u32[]{:S(2)}) async-start(bf16[32,30,128]{2,1,0:T(8,128)(2,1)} %pack.1), calls=%async_computation | async-start | bytes 524288 | tf_op jit(solution)/shard_map/all_to_all | solution.py:333
  41.8 7.4 %collective-permute-start.2 = (bf16[128,768]{1,0:T(8,128)(2,1)S(1)}, bf16[128,768]{1,0:T(8,128)(2,1)S(1)}, u32[]{:S(2)}, u32[]{:S(2)}) collective-permute-start(bf16[128,768]{1,0:T(8,128)(2,1)S(1)} %reshape.50.vert_ref.refs_0_), channel_id=1, source_target_pairs={{0,32},{32,0},{1,33},{33,1},{2,34},{34,2},{3,35},{35,3},{4,36},{36... | collective-permute-start | bytes 589832 | tf_op jit(solution)/shard_map/ppermute | solution.py:336
